TPU v7x, 32 devices: a whole 2x2x4 slice. The times are simulated.
32 devices in a mesh: date: 4 (over y, x), pix: 4 (over z), tile: 2 (over core).
Axes of the slice: x: 2, y: 2, z: 4, core: 2. Of those that a mesh axis runs over, the one named last changes fastest.
Arguments:
- reflectance: float32 [32, 7, 65536], P('date', None, ('tile', 'pix')), parts along dimension 2, may hold values from -6 to 6
- validity: int32 [32, 65536], P('date', ('tile', 'pix')), parts along dimension 1, may hold values from 0 to 1, as said below
- day_number: int32 [32], P('date'), may hold values from 1 to 63, as said below
Outputs:
- filled: float32 [32, 7, 65536], P('date', None, ('tile', 'pix')), parts along dimension 2
There are 2 independent parts, one for each index of `tile`. A program takes and returns all parts, laid end to end along the dimension named above; an argument that names none is the same for every part. Nothing has to cross between parts.
Inputs may be any that keep to these rules, and one draw needn't show every extreme that they name: `validity`: 1 marks a usable observation, 0 a rejected one. `day_number`: strictly increasing along the dates, by 1 to 3 days from one date to the next, starting at day 1.
All inputs are finite; a program needn't handle non-finite values.
Results may differ from a plain program's by a relative error of at most 0.0003.
Values sent between devices are 32-bit elements; how exact they have to be, the bound alone decides.
No kernel may reach another device: no remote copies, remote signals or barrier semaphores. Data moves between devices by JAX's collectives and lax.ppermute only.
A program may use at most 64 MiB of HBM per device.

v0:
```python
import jax
import jax.numpy as jnp
from jax import lax
from jax.sharding import PartitionSpec as P

far_day = 1073741824


def pass_forward(earlier, later):
    keep = later[0] >= 0
    return (
        jnp.where(keep, later[0], earlier[0]),
        jnp.where(keep[:, None, :], later[1], earlier[1]),
    )


def pass_backward(earlier, later):
    keep = later[0] < far_day
    return (
        jnp.where(keep, later[0], earlier[0]),
        jnp.where(keep[:, None, :], later[1], earlier[1]),
    )


def scan_block(values, validity, days):
    live = validity > 0
    day_col = jnp.broadcast_to(days[:, None], validity.shape)
    fwd_day, fwd_val = lax.associative_scan(
        pass_forward, (jnp.where(live, day_col, -1), values), axis=0
    )
    bwd_day, bwd_val = lax.associative_scan(
        pass_backward, (jnp.where(live, day_col, far_day), values), reverse=True, axis=0
    )
    return (live, day_col, fwd_day, fwd_val, bwd_day, bwd_val)


def blend(values, live, day_col, fwd_day, fwd_val, bwd_day, bwd_val):
    has_prev = fwd_day >= 0
    has_next = bwd_day < far_day
    inside = has_prev & has_next & jnp.logical_not(live)
    span = jnp.where(inside, bwd_day - fwd_day, 1).astype(jnp.float32)
    weight = (day_col - fwd_day).astype(jnp.float32) / span
    middle = fwd_val + weight[:, None, :] * (bwd_val - fwd_val)
    one_side = jnp.where(
        has_prev[:, None, :],
        fwd_val,
        jnp.where(has_next[:, None, :], bwd_val, jnp.zeros_like(fwd_val)),
    )
    chosen = jnp.where(inside[:, None, :], middle, one_side)
    return jnp.where(live[:, None, :], values, chosen)


def body(reflectance, validity, day_number):
    live, day_col, fwd_day, fwd_val, bwd_day, bwd_val = scan_block(
        reflectance, validity, day_number
    )
    pixels = reflectance.shape[2]
    bands = reflectance.shape[1]
    none_before = jnp.full((pixels,), -1, jnp.int32)
    none_after = jnp.full((pixels,), far_day, jnp.int32)
    blank = jnp.zeros((bands, pixels), jnp.float32)
    own = lax.axis_index("date")
    pf_day = lax.all_gather(fwd_day[-1:], "date", axis=0, tiled=True)
    pf_val = lax.all_gather(fwd_val[-1:], "date", axis=0, tiled=True)
    pb_day = lax.all_gather(bwd_day[:1], "date", axis=0, tiled=True)
    pb_val = lax.all_gather(bwd_val[:1], "date", axis=0, tiled=True)
    rows = lax.broadcasted_iota(jnp.int32, pf_day.shape, 0)
    f_cand = jnp.where(rows < own, pf_day, -1)
    f_best = jnp.maximum(none_before, jnp.max(f_cand, axis=0))
    f_hit = (f_cand == f_best[None]) & (f_cand >= 0)
    f_from = jnp.sum(jnp.where(f_hit[:, None, :], pf_val, 0.0), axis=0)
    f_new = jnp.where((none_before == f_best)[None], blank, f_from)
    b_cand = jnp.where(rows > own, pb_day, far_day)
    b_best = jnp.minimum(none_after, jnp.min(b_cand, axis=0))
    b_hit = (b_cand == b_best[None]) & (b_cand < far_day)
    b_from = jnp.sum(jnp.where(b_hit[:, None, :], pb_val, 0.0), axis=0)
    b_new = jnp.where((none_after == b_best)[None], blank, b_from)
    keep_f = fwd_day >= 0
    fwd_day = jnp.where(keep_f, fwd_day, f_best[None])
    fwd_val = jnp.where(keep_f[:, None, :], fwd_val, f_new[None])
    keep_b = bwd_day < far_day
    bwd_day = jnp.where(keep_b, bwd_day, b_best[None])
    bwd_val = jnp.where(keep_b[:, None, :], bwd_val, b_new[None])
    return blend(reflectance, live, day_col, fwd_day, fwd_val, bwd_day, bwd_val)


def solution(mesh):
    placed = (P("date", None, ("tile", "pix")), P("date", ("tile", "pix")), P("date"))
    return jax.shard_map(
        body,
        mesh=mesh,
        in_specs=placed,
        out_specs=P("date", None, ("tile", "pix")),
        check_vma=False,
    )
```

profile of v0, /device:TPU:0, one launch (start us, length us, event | category | flops | bytes accessed | tf_op | source)
XLA Modules:
  0.0 107.1 jit_solution(546528375903178266)
XLA Ops:
  0.0 1.1 broadcast_select_fusion.4
  6.2 9.9 %all-gather = s32[4,1,8192]{2,1,0:T(1,128)S(1)} all-gather(s32[1,1,8192]{2,1,0:T(1,128)S(1)} %add_bitcast_fusion.1), channel_id=1, replica_groups=mesh['date'=4,'pix'=4,'tile'=2] {'date'}, dimensions={0}, use_global_device_ids=true | all-gather | bytes 163840 | tf_op jit(solution)/shard_map/all_gather | solution.py:63
  18.1 1.6 %slice.209 = s32[4,8192]{1,0:T(4,128)S(1)} reverse(s32[4,8192]{1,0:T(4,128)S(1)} %slice.208), dimensions={0} | reverse | bytes 262144 | tf_op jit(solution)/shard_map/slice | solution.py:31
  21.2 1.6 %slice.205 = s32[3,8192]{1,0:T(4,128)S(1)} reverse(s32[3,8192]{1,0:T(4,128)S(1)} %slice.204), dimensions={0} | reverse | bytes 196608 | tf_op jit(solution)/shard_map/slice | solution.py:31
  22.8 1.6 %slice.207 = s32[4,8192]{1,0:T(4,128)S(1)} reverse(s32[4,8192]{1,0:T(4,128)S(1)} %slice.206), dimensions={0} | reverse | bytes 262144 | tf_op jit(solution)/shard_map/slice | solution.py:31
  29.1 8.4 %all-gather.1 = s32[4,1,8192]{2,1,0:T(1,128)S(1)} all-gather(s32[1,1,8192]{2,1,0:T(1,128)S(1)} %add_bitcast_fusion), channel_id=1, replica_groups=mesh['date'=4,'pix'=4,'tile'=2] {'date'}, dimensions={0}, use_global_device_ids=true | all-gather | bytes 163840 | tf_op jit(solution)/shard_map/all_gather | solution.py:65
  39.5 2.6 %copy.10 = f32[8,7,8192]{2,1,0:T(8,128)S(1)} copy(f32[8,7,8192]{2,0,1:T(8,128)} %param.3) | data formatting | bytes 3670016 | tf_op args[0]
  47.3 1.1 %pad.90 = f32[4,7,8192]{2,1,0:T(8,128)S(1)} pad(f32[2,7,8192]{2,1,0:T(8,128)} %pad_maximum_fusion.2, f32[]{:T(128)} %constant.14.clone.1), padding=0_1_1x0_0_0x0_0_0 | pad | bytes 1376260 | tf_op jit(solution)/shard_map/pad | solution.py:28
  48.4 2.7 %pad.91 = f32[4,7,8192]{2,1,0:T(8,128)} pad(f32[2,7,8192]{2,1,0:T(8,128)} %pad_add_fusion.1, f32[]{:T(128)} %constant.14.clone.1), padding=1_0_1x0_0_0x0_0_0 | pad | bytes 1376260 | tf_op jit(solution)/shard_map/pad | solution.py:28
  51.1 2.4 %add_select_fusion.1 = (f32[3,7,8192]{2,1,0:T(8,128)S(1)}, f32[3,7,8192]{2,1,0:T(8,128)}) fusion(f32[4,7,8192]{2,1,0:T(8,128)} %pad.91, f32[4,7,8192]{2,1,0:T(8,128)S(1)} %pad.90, f32[8,7,8192]{2,1,0:T(8,128)S(1)} %copy.10, pred[3,8192]{1,0:T(4,128)(4,1)S(1)} %broadcast_compare_fusion.6), kind=kLoop, calls=%fused_computation.7 | loop fusion | flops 344064 | bytes 4153344 | tf_op jit(solution)/shard_map/jit(_where)/select_n | solution.py:13
  53.5 1.1 %add.94 = f32[4,7,8192]{2,1,0:T(8,128)} add(f32[4,7,8192]{2,1,0:T(8,128)S(1)} %pad.90, f32[4,7,8192]{2,1,0:T(8,128)S(1)} %copy-done.1) | non-fusion elementwise | flops 229376 | bytes 2752512 | tf_op jit(solution)/shard_map/add | solution.py:28
  54.6 1.1 %pad_maximum_fusion = f32[4,7,8192]{2,1,0:T(8,128)} fusion(f32[3,7,8192]{2,1,0:T(8,128)S(1)} %get-tuple-element.13, f32[1,7,8192]{2,1,0:T(8,128)S(1)} %copy-done.9), kind=kLoop, calls=%fused_computation.1 | loop fusion | flops 229376 | bytes 1835008 | tf_op jit(solution)/shard_map/concatenate | solution.py:28
  58.8 1.1 pad_maximum_fusion.1
  59.9 2.2 %pad.98 = f32[8,7,8192]{2,1,0:T(8,128)S(1)} pad(f32[4,7,8192]{2,1,0:T(8,128)} %pad_maximum_fusion.1, f32[]{:T(128)} %constant.14.clone.1), padding=0_1_1x0_0_0x0_0_0 | pad | bytes 2752516 | tf_op jit(solution)/shard_map/pad | solution.py:31
  62.1 2.9 %pad.99 = f32[8,7,8192]{2,1,0:T(8,128)} pad(f32[4,7,8192]{2,1,0:T(8,128)S(1)} %add.97, f32[]{:T(128)} %constant.14.clone.1), padding=1_0_1x0_0_0x0_0_0 | pad | bytes 2752516 | tf_op jit(solution)/shard_map/pad | solution.py:31
  64.9 1.0 slice_add_fusion
  65.9 3.2 %add.98 = f32[8,7,8192]{2,1,0:T(8,128)} add(f32[8,7,8192]{2,1,0:T(8,128)S(1)} %pad.98, f32[8,7,8192]{2,1,0:T(8,128)} %pad.99) | non-fusion elementwise | flops 458752 | bytes 5505024 | tf_op jit(solution)/shard_map/add | solution.py:31
  69.1 12.3 %all_gather.15 = f32[4,7,8192]{2,1,0:T(8,128)S(1)} all-gather(f32[1,7,8192]{2,1,0:T(8,128)S(1)} %slice_add_fusion), channel_id=1, replica_groups=mesh['date'=4,'pix'=4,'tile'=2] {'date'}, dimensions={0}, use_global_device_ids=true | all-gather | bytes 1146880 | tf_op jit(solution)/shard_map/all_gather | solution.py:66
  82.4 2.2 %pad.92 = f32[8,7,8192]{2,1,0:T(8,128)S(1)} pad(f32[4,7,8192]{2,1,0:T(8,128)} %pad_maximum_fusion, f32[]{:T(128)} %constant.14.clone.1), padding=0_1_1x0_0_0x0_0_0 | pad | bytes 2752516 | tf_op jit(solution)/shard_map/pad | solution.py:28
  84.6 2.9 %pad.93 = f32[8,7,8192]{2,1,0:T(8,128)} pad(f32[4,7,8192]{2,1,0:T(8,128)S(1)} %copy-done.3, f32[]{:T(128)} %constant.14.clone.1), padding=1_0_1x0_0_0x0_0_0 | pad | bytes 2752516 | tf_op jit(solution)/shard_map/pad | solution.py:28
  87.5 1.1 %slice_add_fusion.1 = f32[1,7,8192]{2,1,0:T(8,128)S(1)} fusion(f32[8,7,8192]{2,1,0:T(8,128)} %pad.93, f32[8,7,8192]{2,1,0:T(8,128)S(1)} %pad.92), kind=kLoop, calls=%fused_computation.25 | loop fusion | flops 57344 | bytes 688128 | tf_op jit(solution)/shard_map/add | solution.py:28
  88.6 11.5 %all_gather.14 = f32[4,7,8192]{2,1,0:T(8,128)S(1)} all-gather(f32[1,7,8192]{2,1,0:T(8,128)S(1)} %slice_add_fusion.1), channel_id=1, replica_groups=mesh['date'=4,'pix'=4,'tile'=2] {'date'}, dimensions={0}, use_global_device_ids=true | all-gather | bytes 1146880 | tf_op jit(solution)/shard_map/all_gather | solution.py:64
  101.2 3.7 %select_select_fusion = f32[8,7,8192]{2,1,0:T(8,128)S(1)} fusion(f32[8,7,8192]{2,1,0:T(8,128)} %add.98, f32[8,7,8192]{2,1,0:T(8,128)S(1)} %pad.92, f32[8,7,8192]{2,1,0:T(8,128)S(1)} %copy-done, f32[7,8192]{1,0:T(8,128)} %broadcast_select_fusion.1, f32[8,8192]{1,0:T(8,128)S(1)} %copy-done.7, f32[7,8192]{1,0:T(8,128)S(1)} %broadcast_select_fusion.2, ...), kind=kLoop, calls=%fused_computation | loop fusion | flops 4587520 | bytes 10289152 | tf_op jit(solution)/shard_map/jit(_where)/select_n | solution.py:50
  104.8 2.3 %copy.11 = f32[8,7,8192]{2,0,1:T(8,128)} copy(f32[8,7,8192]{2,1,0:T(8,128)S(1)} %select_select_fusion) | data formatting | bytes 3670016 | tf_op jit(solution)/shard_map/jit(_where)/select_n | solution.py:50
  (111 shorter events, 25.1 us)
Async XLA Ops:
  5.3 11.9 %copy-start.11 = (s32[8]{0:T(128)S(1)}, s32[8]{0:T(128)}, u32[]{:S(2)}) copy-start(s32[8]{0:T(128)} %param.5) | copy-start | bytes 100
  51.1 2.4 %copy-start.1 = (f32[4,7,8192]{2,1,0:T(8,128)S(1)}, f32[4,7,8192]{2,1,0:T(8,128)}, u32[]{:S(2)}) copy-start(f32[4,7,8192]{2,1,0:T(8,128)} %pad.91) | copy-start | bytes 2752516
  53.5 1.1 %copy-start.9 = (f32[1,7,8192]{2,1,0:T(8,128)S(1)}, f32[1,7,8192]{2,1,0:T(8,128)}, u32[]{:S(2)}) copy-start(f32[1,7,8192]{2,1,0:T(8,128)} %get-tuple-element.11) | copy-start | bytes 688132
  53.5 2.2 %copy-start.6 = (f32[2,7,8192]{2,1,0:T(8,128)S(1)}, f32[2,7,8192]{2,1,0:T(8,128)}, u32[]{:S(2)}) copy-start(f32[2,7,8192]{2,1,0:T(8,128)} %pad_maximum_fusion.3) | copy-start | bytes 1376260
  54.6 1.2 %copy-start.5 = (f32[2,7,8192]{2,1,0:T(8,128)S(1)}, f32[2,7,8192]{2,1,0:T(8,128)}, u32[]{:S(2)}) copy-start(f32[2,7,8192]{2,1,0:T(8,128)} %pad_add_fusion) | copy-start | bytes 1376260
  55.8 1.1 %copy-start.4 = (f32[3,7,8192]{2,1,0:T(8,128)S(1)}, f32[3,7,8192]{2,1,0:T(8,128)}, u32[]{:S(2)}) copy-start(f32[3,7,8192]{2,1,0:T(8,128)} %get-tuple-element.14) | copy-start | bytes 2064388
  57.9 1.0 copy-start.8
  65.9 15.5 %copy-start.10 = (pred[4,8192]{1,0:T(4,128)(4,1)S(1)}, pred[4,8192]{1,0:T(4,128)(4,1)}, u32[]{:S(2)}) copy-start(pred[4,8192]{1,0:T(4,128)(4,1)} %compare_and_fusion) | copy-start | bytes 98308
  81.6 2.9 %copy-start.3 = (f32[4,7,8192]{2,1,0:T(8,128)S(1)}, f32[4,7,8192]{2,1,0:T(8,128)}, u32[]{:S(2)}) copy-start(f32[4,7,8192]{2,1,0:T(8,128)} %add.94) | copy-start | bytes 2752516
  84.6 16.6 %copy-start.7 = (f32[8,8192]{1,0:T(8,128)S(1)}, f32[8,8192]{1,0:T(8,128)}, u32[]{:S(2)}) copy-start(f32[8,8192]{1,0:T(8,128)} %get-tuple-element.5) | copy-start | bytes 786436
  87.5 13.7 %copy-start = (f32[8,7,8192]{2,1,0:T(8,128)S(1)}, f32[8,7,8192]{2,1,0:T(8,128)}, u32[]{:S(2)}) copy-start(f32[8,7,8192]{2,1,0:T(8,128)} %pad.93) | copy-start | bytes 5505028
  87.5 13.7 %copy-start.2 = (f32[8,7,8192]{2,0,1:T(8,128)S(1)}, f32[8,7,8192]{2,0,1:T(8,128)}, u32[]{:S(2)}) copy-start(f32[8,7,8192]{2,0,1:T(8,128)} %param.3) | copy-start | bytes 5505028
where the time goes:
time: 108 us; the launch traced here: 107 us
  blocking collectives  42.2 us (39%)
  local copies, waits for them, and re-layouts  35.1 us (32%)
  other arithmetic  29.2 us (27%)
    all_gather x1, blocking collectives, body(): pb_val = lax.all_gather(bwd_val[:1], 'date', axis=0, tiled=True)  12.3 us
    all_gather x1, blocking collectives, body(): pf_val = lax.all_gather(fwd_val[-1:], 'date', axis=0, tiled=True)  11.5 us
    all_gather x1, blocking collectives, body(): pf_day = lax.all_gather(fwd_day[-1:], 'date', axis=0, tiled=True)  9.94 us
    pad x8, local copies, waits for them, and re-layouts, scan_block(): lax.associative_scan(pass_forward, (jnp.where(live, day_col, -1), values)...  9.27 us
    all_gather x1, blocking collectives, body(): pb_day = lax.all_gather(bwd_day[:1], 'date', axis=0, tiled=True)  8.42 us
    slice x9, local copies, waits for them, and re-layouts, scan_block(): lax.associative_scan(pass_backward, (jnp.where(live, day_col, far_day), v...  8.14 us
    pad x8, local copies, waits for them, and re-layouts, scan_block(): lax.associative_scan(pass_backward, (jnp.where(live, day_col, far_day), v...  5.63 us
    add x7, other arithmetic, scan_block(): lax.associative_scan(pass_backward, (jnp.where(live, day_col, far_day), v...  5.24 us

commit v1 on v0

v1 whole, which is shorter than its diff:
```python
import functools

import jax
import jax.numpy as jnp
from jax import lax
from jax.experimental import pallas as pl
from jax.experimental.pallas import tpu as pltpu
from jax.sharding import PartitionSpec as P

far_day = 1073741824.0
LANES = 128


def day_column(days_ref, count):
    rows = lax.broadcasted_iota(jnp.int32, (count, LANES), 0)
    col = jnp.zeros((count, LANES), jnp.float32)
    for t in range(count):
        col = jnp.where(rows == t, days_ref[t].astype(jnp.float32), col)
    return rows, col


def pick(x, pos):
    return jnp.take_along_axis(x, pos, axis=0)


def running(pos, rows, count, forward):
    step = 1
    while step < count:
        shift = step if forward else count - step
        moved = pltpu.roll(pos, shift, 0)
        if forward:
            pos = jnp.maximum(pos, jnp.where(rows >= step, moved, -1))
        else:
            pos = jnp.minimum(pos, jnp.where(rows < count - step, moved, count))
        step *= 2
    return pos


def whole(pos, count, last):
    step = 1
    while step < count:
        moved = pltpu.roll(pos, step, 0)
        pos = jnp.maximum(pos, moved) if last else jnp.minimum(pos, moved)
        step *= 2
    return pos


def summary_kernel(tops, me_ref, days_ref, refl_ref, valid_ref, *out_refs):
    bands, count, width = refl_ref.shape
    rows, day_col = day_column(days_ref, count)
    out_rows = lax.broadcasted_iota(jnp.int32, (bands + 1, LANES), 0)
    me = me_ref[0]
    wants_last = [lax.rem(lax.div(me, 1 << t), 2) == 0 for t in tops]
    for i in range(width // LANES):
        cols = pl.ds(i * LANES, LANES)
        live = valid_ref[:, cols] > 0
        last = whole(jnp.where(live, rows, -1), count, True)
        first = whole(jnp.where(live, rows, count), count, False)
        found = last >= 0
        for t, out_ref in zip(wants_last, out_refs):
            pos = jnp.where(found, jnp.where(t, last, first), 0)
            got = jnp.where(found, pick(day_col, pos), 0.0)
            for b in range(bands):
                got = jnp.where(out_rows == b, pick(refl_ref[b, :, cols], pos), got)
            out_ref[:, cols] = got


def fill_kernel(tops, me_ref, days_ref, refl_ref, valid_ref, *refs):
    got_refs, out_ref = refs[:-1], refs[-1]
    bands, count, width = refl_ref.shape
    rows, day_col = day_column(days_ref, count)
    me = me_ref[0]
    is_prev = [lax.rem(lax.div(me, 1 << t), 2) == 1 for t in tops]
    shape = (bands + 1, LANES)
    for i in range(width // LANES):
        cols = pl.ds(i * LANES, LANES)
        live = valid_ref[:, cols] > 0
        prev_pos = running(jnp.where(live, rows, -1), rows, count, True)
        next_pos = running(jnp.where(live, rows, count), rows, count, False)
        prev_in = prev_pos >= 0
        next_in = next_pos < count
        prev_pos = jnp.maximum(prev_pos, 0)
        next_pos = jnp.minimum(next_pos, count - 1)
        before = jnp.zeros(shape, jnp.float32)
        after = jnp.zeros(shape, jnp.float32)
        before_day = jnp.zeros(shape, jnp.float32)
        after_day = jnp.full(shape, far_day, jnp.float32)
        for earlier, got_ref in zip(is_prev, got_refs):
            got = got_ref[:, cols]
            day = jnp.broadcast_to(got[bands:], shape)
            day_p = jnp.where(earlier, day, 0.0)
            day_n = jnp.where(jnp.logical_or(earlier, day <= 0.0), far_day, day)
            before = jnp.where(day_p > before_day, got, before)
            after = jnp.where(day_n < after_day, got, after)
            before_day = jnp.maximum(before_day, day_p)
            after_day = jnp.minimum(after_day, day_n)
        prev_day = jnp.where(prev_in, pick(day_col, prev_pos), before_day[:1])
        next_day = jnp.where(next_in, pick(day_col, next_pos), after_day[:1])
        has_prev = prev_day > 0.0
        has_next = next_day < far_day
        both = jnp.logical_and(has_prev, has_next)
        span = jnp.maximum(jnp.where(both, next_day - prev_day, 1.0), 1.0)
        weight = jnp.where(
            both, (day_col - prev_day) / span, jnp.where(has_prev, 0.0, 1.0)
        )
        for b in range(bands):
            x = refl_ref[b, :, cols]
            prev = jnp.where(prev_in, pick(x, prev_pos), before[b : b + 1])
            nxt = jnp.where(next_in, pick(x, next_pos), after[b : b + 1])
            out_ref[b, :, cols] = prev + weight * (nxt - prev)


def body(devices, width, reflectance, validity, day_number):
    count, bands, pixels = reflectance.shape
    refl = jnp.transpose(reflectance, (1, 0, 2))
    me = lax.axis_index("date")
    me_arr = me.reshape(1).astype(jnp.int32)
    bits = devices.bit_length() - 1
    smem = pl.BlockSpec(memory_space=pltpu.SMEM)
    stack = pl.BlockSpec((bands, count, width), lambda i: (0, 0, i))
    flat = pl.BlockSpec((count, width), lambda i: (0, i))
    packet = pl.BlockSpec((bands + 1, width), lambda i: (0, i))
    params = pltpu.CompilerParams(vmem_limit_bytes=24 << 20)
    sends = pl.pallas_call(
        functools.partial(summary_kernel, list(range(bits))),
        grid=(pixels // width,),
        in_specs=[smem, smem, stack, flat],
        out_specs=[packet] * bits,
        out_shape=[jax.ShapeDtypeStruct((bands + 1, pixels), jnp.float32)] * bits,
        compiler_params=params,
        name="summary",
    )(me_arr, day_number, refl, validity)
    gots, tops = [], []
    for k in range(1, devices):
        top = k.bit_length() - 1
        pairs = [(d, d ^ k) for d in range(devices)]
        gots.append(lax.ppermute(sends[top], "date", pairs))
        tops.append(top)
    out = pl.pallas_call(
        functools.partial(fill_kernel, tops),
        grid=(pixels // width,),
        in_specs=[smem, smem, stack, flat] + [packet] * len(gots),
        out_specs=stack,
        out_shape=jax.ShapeDtypeStruct((bands, count, pixels), jnp.float32),
        compiler_params=params,
        name="fill",
    )(me_arr, day_number, refl, validity, *gots)
    return jnp.transpose(out, (1, 0, 2))


def solution(mesh):
    placed = (P("date", None, ("tile", "pix")), P("date", ("tile", "pix")), P("date"))
    return jax.shard_map(
        functools.partial(body, mesh.shape["date"], 1024),
        mesh=mesh,
        in_specs=placed,
        out_specs=P("date", None, ("tile", "pix")),
        check_vma=False,
    )
```

time: 108 us -> 26.7 us (0.25)
  blocking collectives: 42.2 us -> 0 us
  local copies, waits for them, and re-layouts: 35.1 us -> 3.1 us
  other arithmetic: 29.2 us -> 0 us
  waiting for transfers between devices: 0 us -> 13.1 us
  Pallas kernels: 0 us -> 5.75 us
  starting transfers between devices: 0 us -> 4.57 us
    all_gather x4 -> x0, blocking collectives: 42.2 us -> none  [the longest x1 12.3 us: body(): pb_val = lax.all_gather(bwd_val[:1], 'date', axis=0, tiled=True)]
    pad x16 -> x0, local copies, waits for them, and re-layouts: 14.9 us -> none  [the longest x8 9.27 us: scan_block(): lax.associative_scan(pass_forward, (jnp.where(live, day_col, -1), values)...]
    ppermute x0 -> x3, waiting for transfers between devices: none -> 13.1 us  [body(): gots.append(lax.ppermute(sends[top], 'date', pairs))]
    slice x16 -> x0, local copies, waits for them, and re-layouts: 12.6 us -> none  [the longest x9 8.14 us: scan_block(): lax.associative_scan(pass_backward, (jnp.where(live, day_col, far_day), v...]
    select_n x19 -> x0, other arithmetic: 10 us -> none  [the longest x1 3.67 us: blend(): return jnp.where(live[:, None, :], values, chosen)]
    add x12 -> x0, other arithmetic: 8.4 us -> none  [the longest x7 5.24 us: scan_block(): lax.associative_scan(pass_backward, (jnp.where(live, day_col, far_day), v...]
    pallas_call x0 -> x2, Pallas kernels: none -> 5.75 us  [the longest x1 4.25 us: body(): pl.pallas_call(functools.partial(fill_kernel, tops), grid=(pixels // widt...]
    ppermute x0 -> x3, starting transfers between devices: none -> 4.57 us  [body(): gots.append(lax.ppermute(sends[top], 'date', pairs))]
  transfers between devices with their start and end apart: 0 -> 3, of which waited for: 0 -> 3; matrix products, arithmetic and copies ran while one was open for 0% -> 0% of each run, Pallas kernels for 0% -> 0%
where the time goes in v1:
time: 26.7 us; the launch traced here: 26.5 us
  waiting for transfers between devices  13.1 us (49%)
  Pallas kernels  5.75 us (22%)
  starting transfers between devices  4.57 us (17%)
  local copies, waits for them, and re-layouts  3.1 us (12%)
    ppermute x3, waiting for transfers between devices, body(): gots.append(lax.ppermute(sends[top], 'date', pairs))  13.1 us
    ppermute x3, starting transfers between devices, body(): gots.append(lax.ppermute(sends[top], 'date', pairs))  4.57 us
    pallas_call x1, Pallas kernels, body(): pl.pallas_call(functools.partial(fill_kernel, tops), grid=(pixels // widt...  4.25 us
    unnamed x6, local copies, waits for them, and re-layouts  3.1 us
    pallas_call x1, Pallas kernels, body(): pl.pallas_call(functools.partial(summary_kernel, list(range(bits))), grid...  1.5 us
  transfers between devices with their start and end apart: 3, of which 3 were waited for; matrix products, arithmetic and copies ran while one was open for 0% of the time, Pallas kernels for 0%

profile of v1, /device:TPU:0, one launch (start us, length us, event | category | flops | bytes accessed | tf_op | source)
XLA Modules:
  0.0 26.5 jit_solution(14427808515972224411)
XLA Ops:
  0.0 0.0 copy-start
  0.0 1.5 %copy-done = f32[8,7,8192]{2,0,1:T(8,128)S(1)} copy-done((f32[8,7,8192]{2,0,1:T(8,128)S(1)}, f32[8,7,8192]{2,0,1:T(8,128)}, u32[]{:S(2)}) %copy-start) | copy-done | bytes 1835032
  1.5 0.0 copy-start.1
  1.5 0.9 %copy-done.1 = s32[8,8192]{1,0:T(8,128)S(1)} copy-done((s32[8,8192]{1,0:T(8,128)S(1)}, s32[8,8192]{1,0:T(8,128)}, u32[]{:S(2)}) %copy-start.1) | copy-done | bytes 262168
  2.5 0.0 copy-start.2
  2.5 0.7 %copy-done.2 = s32[8]{0:T(128)S(1)} copy-done((s32[8]{0:T(128)S(1)}, s32[8]{0:T(128)}, u32[]{:S(2)}) %copy-start.2) | copy-done | bytes 56
  3.1 1.5 %summary.1 = (f32[8,8192]{1,0:T(8,128)S(1)}, f32[8,8192]{1,0:T(8,128)S(1)}) custom-call(s32[1]{0:T(128)} %bitcast.me_ref, s32[8]{0:T(128)S(1)} %copy-done.2, f32[7,8,8192]{2,1,0:T(8,128)S(1)} %bitcast.3, s32[8,8192]{1,0:T(8,128)S(1)} %copy-done.1), custom_call_target="tpu_custom_call" | custom-call | tf_op jit(solution)/shard_map/summary/pallas_call | solution.py:124
  4.6 3.0 %collective-permute-start = (f32[8,8192]{1,0:T(8,128)S(1)}, f32[8,8192]{1,0:T(8,128)S(1)}, u32[]{:S(2)}, u32[]{:S(2)}) collective-permute-start(f32[8,8192]{1,0:T(8,128)S(1)} %get-tuple-element.7), channel_id=1, source_target_pairs={{0,8},{8,0},{16,24},{24,16},{1,9},{9,1},{17,25},{25,17},{2,10},{10... | collective-permute-start | bytes 786440 | tf_op jit(solution)/shard_map/ppermute | solution.py:137
  7.6 1.5 %collective-permute-start.2 = (f32[8,8192]{1,0:T(8,128)S(1)}, f32[8,8192]{1,0:T(8,128)S(1)}, u32[]{:S(2)}, u32[]{:S(2)}) collective-permute-start(f32[8,8192]{1,0:T(8,128)S(1)} %get-tuple-element.8), channel_id=1, source_target_pairs={{0,24},{8,16},{16,8},{24,0},{1,25},{9,17},{17,9},{25,1},{2,26},{10... | collective-permute-start | bytes 786440 | tf_op jit(solution)/shard_map/ppermute | solution.py:137
  9.1 0.1 collective-permute-start.1
  9.2 5.6 %collective-permute-done.refs_0_ = f32[8,8192]{1,0:T(8,128)S(1)} collective-permute-done((f32[8,8192]{1,0:T(8,128)S(1)}, f32[8,8192]{1,0:T(8,128)S(1)}, u32[]{:S(2)}, u32[]{:S(2)}) %collective-permute-start) | collective-permute-done | bytes 262176 | tf_op jit(solution)/shard_map/ppermute | solution.py:137
  14.8 6.1 %collective-permute-done.2.refs_2_ = f32[8,8192]{1,0:T(8,128)S(1)} collective-permute-done((f32[8,8192]{1,0:T(8,128)S(1)}, f32[8,8192]{1,0:T(8,128)S(1)}, u32[]{:S(2)}, u32[]{:S(2)}) %collective-permute-start.2) | collective-permute-done | bytes 262176 | tf_op jit(solution)/shard_map/ppermute | solution.py:137
  20.9 1.4 %collective-permute-done.1.refs_1_ = f32[8,8192]{1,0:T(8,128)S(1)} collective-permute-done((f32[8,8192]{1,0:T(8,128)S(1)}, f32[8,8192]{1,0:T(8,128)S(1)}, u32[]{:S(2)}, u32[]{:S(2)}) %collective-permute-start.1) | collective-permute-done | bytes 262176 | tf_op jit(solution)/shard_map/ppermute | solution.py:137
  22.2 4.3 %fill.1 = f32[7,8,8192]{2,1,0:T(8,128)} custom-call(s32[1]{0:T(128)} %bitcast.me_ref, s32[8]{0:T(128)S(1)} %copy-done.2, f32[7,8,8192]{2,1,0:T(8,128)S(1)} %bitcast.4, s32[8,8192]{1,0:T(8,128)S(1)} %copy-done.1, f32[8,8192]{1,0:T(8,128)S(1)} %collective-permute-done.refs_0_, f32[8,8192]{1,0:T(8,128)S(1)} %collective-permute-done.1.refs_1_, ...), custom_call_target="tpu_custom_call" | custom-call | tf_op jit(solution)/shard_map/fill/pallas_call | solution.py:139
Async XLA Ops:
  0.0 1.5 %copy-start = (f32[8,7,8192]{2,0,1:T(8,128)S(1)}, f32[8,7,8192]{2,0,1:T(8,128)}, u32[]{:S(2)}) copy-start(f32[8,7,8192]{2,0,1:T(8,128)} %param.3) | copy-start | bytes 5505028
  1.5 0.9 %copy-start.1 = (s32[8,8192]{1,0:T(8,128)S(1)}, s32[8,8192]{1,0:T(8,128)}, u32[]{:S(2)}) copy-start(s32[8,8192]{1,0:T(8,128)} %valid_ref.3) | copy-start | bytes 786436
  2.5 0.7 %copy-start.2 = (s32[8]{0:T(128)S(1)}, s32[8]{0:T(128)}, u32[]{:S(2)}) copy-start(s32[8]{0:T(128)} %days_ref.3) | copy-start | bytes 100
  4.6 10.2 %collective-permute-start = (f32[8,8192]{1,0:T(8,128)S(1)}, f32[8,8192]{1,0:T(8,128)S(1)}, u32[]{:S(2)}, u32[]{:S(2)}) collective-permute-start(f32[8,8192]{1,0:T(8,128)S(1)} %get-tuple-element.7), channel_id=1, source_target_pairs={{0,8},{8,0},{16,24},{24,16},{1,9},{9,1},{17,25},{25,17},{2,10},{10... | collective-permute-start | bytes 786440 | tf_op jit(solution)/shard_map/ppermute | solution.py:137
  7.6 13.2 %collective-permute-start.2 = (f32[8,8192]{1,0:T(8,128)S(1)}, f32[8,8192]{1,0:T(8,128)S(1)}, u32[]{:S(2)}, u32[]{:S(2)}) collective-permute-start(f32[8,8192]{1,0:T(8,128)S(1)} %get-tuple-element.8), channel_id=1, source_target_pairs={{0,24},{8,16},{16,8},{24,0},{1,25},{9,17},{17,9},{25,1},{2,26},{10... | collective-permute-start | bytes 786440 | tf_op jit(solution)/shard_map/ppermute | solution.py:137
  9.1 13.1 %collective-permute-start.1 = (f32[8,8192]{1,0:T(8,128)S(1)}, f32[8,8192]{1,0:T(8,128)S(1)}, u32[]{:S(2)}, u32[]{:S(2)}) collective-permute-start(f32[8,8192]{1,0:T(8,128)S(1)} %get-tuple-element.8), channel_id=1, source_target_pairs={{0,16},{8,24},{16,0},{24,8},{1,17},{9,25},{17,1},{25,9},{2,18},{10... | collective-permute-start | bytes 786440 | tf_op jit(solution)/shard_map/ppermute | solution.py:137

commit v2 on v0

v2 whole, which is shorter than its diff:
```python
import functools

import jax
import jax.numpy as jnp
from jax import lax
from jax.experimental import pallas as pl
from jax.experimental.pallas import tpu as pltpu
from jax.sharding import PartitionSpec as P

LANES = 128
TOP = 1048576.0
VMEM = pl.BlockSpec(memory_space=pltpu.VMEM)
HBM = pl.BlockSpec(memory_space=pltpu.HBM)
PARAMS = pltpu.CompilerParams(vmem_limit_bytes=16 << 20)


def f32(*shape):
    return jax.ShapeDtypeStruct(shape, jnp.float32)


def pick(x, pos):
    return jnp.take_along_axis(x, pos, axis=0, mode="promise_in_bounds")


def sublane_max(x, count):
    step = 1
    while step < count:
        x = jnp.maximum(x, pltpu.roll(x, step, 0))
        step *= 2
    return x


def running(pos, rows, count, forward):
    step = 1
    while step < count:
        if forward:
            moved = pltpu.roll(pos, step, 0)
            pos = jnp.maximum(pos, jnp.where(rows >= step, moved, -1))
        else:
            moved = pltpu.roll(pos, count - step, 0)
            pos = jnp.minimum(pos, jnp.where(rows < count - step, moved, count))
        step *= 2
    return pos


def span_of(i):
    return pl.ds(pl.multiple_of(i * LANES, LANES), LANES)


def packet_of(values, live, day_col, rows, packet_rows, firsts):
    count = rows.shape[0]
    bands = len(values)
    outs = []
    for first in firsts:
        order = jnp.where(first, count - rows, rows + 1)
        best = sublane_max(jnp.where(live, order, 0), count)
        pos = jnp.where(first, count - best, best - 1) & (count - 1)
        near = jnp.where(first, TOP - day_col, day_col)
        got = pick(near, pos)
        for b in range(bands):
            got = jnp.where(packet_rows == b, pick(values[b], pos), got)
        outs.append(jnp.where(best > 0, got, 0.0))
    return outs


def bit_of(me, t):
    return lax.rem(lax.div(me, 1 << t), 2) == 1


def flags():
    me = lax.axis_index("date")
    return bit_of(me, 0), bit_of(me, 1), jnp.logical_or(me == 1, me == 2)


def tile_rows(bands, count):
    rows = lax.broadcasted_iota(jnp.int32, (count, LANES), 0)
    packet_rows = lax.broadcasted_iota(jnp.int32, (bands + 1, LANES), 0)
    return rows, packet_rows


def load_kernel(piece, bits, days_in, refl_in, valid_in, refl, valid, day_out, *rest):
    sends, (days, day_sem, sems) = rest[: len(bits)], rest[len(bits) :]
    bands, count, pixels = refl.shape
    half = sends[0].shape[1]
    day_copy = pltpu.make_async_copy(days_in, days, day_sem)
    day_copy.start()
    copies = []
    at = 0
    while at < pixels:
        width = piece if at < half else pixels - half
        cols = pl.ds(at, width)
        k = len(copies)
        pair = (
            pltpu.make_async_copy(
                valid_in.at[:, cols], valid.at[:, cols], sems.at[2 * k]
            ),
            pltpu.make_async_copy(
                refl_in.at[:, :, cols], refl.at[:, :, cols], sems.at[2 * k + 1]
            ),
        )
        for c in pair:
            c.start()
        copies.append(pair)
        at += width
    rows, packet_rows = tile_rows(bands, count)
    me = lax.axis_index("date")
    firsts = [bit_of(me, t) for t in bits]
    day_copy.wait()
    day_col = jnp.zeros((count, LANES), jnp.float32)
    for t in range(count):
        day_col = jnp.where(rows == t, days[t].astype(jnp.float32), day_col)
    day_out[...] = day_col
    for k in range(half // piece):
        for c in copies[k]:
            c.wait()

        @pl.loop(0, piece // LANES // 4)
        def _(j):
            for u in range(4):
                cols = span_of(k * (piece // LANES) + j * 4 + u)
                live = valid[:, cols] > 0
                values = [refl[b, :, cols] for b in range(bands)]
                packets = packet_of(values, live, day_col, rows, packet_rows, firsts)
                for send, packet in zip(sends, packets):
                    send[:, cols] = packet

    for pair in copies[half // piece :]:
        for c in pair:
            c.wait()


def second_kernel(refl, valid, day_in, sx_first, sy, sx, side):
    bands, count, pixels = refl.shape
    half = pixels // 2
    rows, packet_rows = tile_rows(bands, count)
    odd, upper, inner = flags()
    day_col = day_in[...]

    @pl.loop(0, half // LANES // 4)
    def _(j):
        for u in range(4):
            cols = span_of(j * 4 + u)
            far = span_of(half // LANES + j * 4 + u)
            live = valid[:, far] > 0
            values = [refl[b, :, far] for b in range(bands)]
            a, b = packet_of(values, live, day_col, rows, packet_rows, (upper, odd))
            sy[:, cols] = a
            sx[:, cols] = b
            side[:, cols] = jnp.where(inner, sx_first[:, cols], b)


def nearness(packet):
    return jnp.broadcast_to(packet[packet.shape[0] - 1 :], packet.shape)


def join_near_kernel(own, got, out):
    @pl.loop(0, own.shape[1] // LANES // 4)
    def _(j):
        for u in range(4):
            cols = span_of(j * 4 + u)
            a, b = own[:, cols], got[:, cols]
            out[:, cols] = jnp.where(nearness(a) >= nearness(b), a, b)


def join_own_kernel(own, got, out):
    _, _, inner = flags()

    @pl.loop(0, own.shape[1] // LANES // 4)
    def _(j):
        for u in range(4):
            cols = span_of(j * 4 + u)
            a, b = own[:, cols], got[:, cols]
            use = jnp.logical_and(inner, nearness(a) > 0.0)
            out[:, cols] = jnp.where(use, a, b)


def merge_first(refs, cols):
    _, upper, inner = flags()
    main, side, other = (r[:, cols] for r in refs)
    side = jnp.where(inner, 0.0, side)
    other = jnp.where(inner, other, 0.0)
    near = jnp.where(nearness(main) >= nearness(side), main, side)
    return jnp.where(upper, near, other), jnp.where(upper, other, near)


def merge_second(refs, cols):
    _, upper, inner = flags()
    main, more, side = (r[:, cols] for r in refs)
    other = jnp.where(inner, side, 0.0)
    near = jnp.where(nearness(main) >= nearness(more), main, more)
    return jnp.where(upper, near, other), jnp.where(upper, other, near)


def merge_all(bits, refs, cols):
    me = lax.axis_index("date")
    before = jnp.zeros((refs[0].shape[0], LANES), jnp.float32)
    after = before
    for t, ref in zip(bits, refs):
        got = ref[:, cols]
        prev = jnp.where(bit_of(me, t), got, 0.0)
        nxt = jnp.where(bit_of(me, t), 0.0, got)
        before = jnp.where(nearness(prev) > nearness(before), prev, before)
        after = jnp.where(nearness(nxt) > nearness(after), nxt, after)
    return before, after


def fill_kernel(start, width, piece, packets, merge, refl, valid, day_in, *rest):
    gots = rest[:packets]
    out, buf, sems = rest[-3:]
    bands, count, _ = refl.shape
    rows, _ = tile_rows(bands, count)
    day_col = day_in[...]
    copies = []
    for k in range(width // piece):

        @pl.loop(0, piece // LANES // 4)
        def _(j):
            for u in range(4):
                i = k * (piece // LANES) + j * 4 + u
                cols = span_of(i)
                far = span_of(start // LANES + i)
                live = valid[:, far] > 0
                prev_pos = running(jnp.where(live, rows, -1), rows, count, True)
                next_pos = running(jnp.where(live, rows, count), rows, count, False)
                prev_in = prev_pos >= 0
                next_in = next_pos < count
                prev_pos = prev_pos & (count - 1)
                next_pos = next_pos & (count - 1)
                before, after = merge(gots, cols)
                prev_day = jnp.where(prev_in, pick(day_col, prev_pos), before[bands:])
                next_day = jnp.where(
                    next_in, pick(day_col, next_pos), TOP - after[bands:]
                )
                has_prev = prev_day > 0.0
                has_next = next_day < TOP
                both = jnp.logical_and(has_prev, has_next)
                span = jnp.maximum(jnp.where(both, next_day - prev_day, 1.0), 1.0)
                weight = jnp.where(
                    both, (day_col - prev_day) / span, jnp.where(has_prev, 0.0, 1.0)
                )
                for b in range(bands):
                    x = refl[b, :, far]
                    prev = jnp.where(prev_in, pick(x, prev_pos), before[b : b + 1])
                    nxt = jnp.where(next_in, pick(x, next_pos), after[b : b + 1])
                    buf[b, :, cols] = prev + weight * (nxt - prev)

        copy = pltpu.make_async_copy(
            buf.at[:, :, pl.ds(k * piece, piece)],
            out.at[:, :, pl.ds(start + k * piece, piece)],
            sems.at[k],
        )
        copy.start()
        copies.append(copy)
    for copy in copies:
        copy.wait()


def fill(name, start, piece, merge, refl, valid, day_col, gots, out=None):
    bands, count, pixels = refl.shape
    width = gots[0].shape[1]
    held = () if out is None else (out,)
    return pl.pallas_call(
        functools.partial(fill_kernel, start, width, piece, len(gots), merge),
        in_specs=[VMEM] * (3 + len(gots)) + [HBM] * len(held),
        out_specs=HBM,
        out_shape=f32(bands, count, pixels),
        input_output_aliases={} if out is None else {3 + len(gots): 0},
        scratch_shapes=[
            pltpu.VMEM((bands, count, width), jnp.float32),
            pltpu.SemaphoreType.DMA((width // piece,)),
        ],
        compiler_params=PARAMS,
        name=name,
    )(refl, valid, day_col, *gots, *held)


def load(piece, width, bits, days, stack, validity):
    bands, count, pixels = stack.shape
    args = (pltpu.with_memory_space_constraint(a, pltpu.HBM) for a in (days, stack, validity))
    return pl.pallas_call(
        functools.partial(load_kernel, piece, bits),
        in_specs=[HBM] * 3,
        out_specs=[VMEM] * (3 + len(bits)),
        out_shape=[
            f32(bands, count, pixels),
            jax.ShapeDtypeStruct((count, pixels), jnp.int32),
            f32(count, LANES),
        ]
        + [f32(bands + 1, width)] * len(bits),
        scratch_shapes=[
            pltpu.SMEM((count,), jnp.int32),
            pltpu.SemaphoreType.DMA,
            pltpu.SemaphoreType.DMA((2 * (width // piece + 1),)),
        ],
        compiler_params=PARAMS,
        name="load",
    )(*args)


def body_any(devices, reflectance, validity, day_number):
    pixels = reflectance.shape[2]
    piece = pixels // 8
    stack = jnp.transpose(reflectance, (1, 0, 2))
    bits = list(range((devices - 1).bit_length()))
    refl, valid, day_col, *sends = load(piece, pixels, bits, day_number, stack, validity)
    gots, tops = [], []
    for k in range(1, 1 << len(bits)):
        pairs = [(d, d ^ k) for d in range(devices) if d ^ k < devices]
        tops.append(k.bit_length() - 1)
        gots.append(lax.ppermute(sends[tops[-1]], "date", pairs))
    merge = functools.partial(merge_all, tops)
    out = fill("fill", 0, piece, merge, refl, valid, day_col, gots)
    return jnp.transpose(out, (1, 0, 2))


def body(reflectance, validity, day_number):
    count, bands, pixels = reflectance.shape
    half = pixels // 2
    piece = half // 4
    stack = jnp.transpose(reflectance, (1, 0, 2))
    packet = f32(bands + 1, half)
    across = lambda x: lax.ppermute(x, "date", [(d, d ^ 1) for d in range(4)])
    along = lambda x: lax.ppermute(x, "date", [(d, d ^ 2) for d in range(4)])

    refl, valid, day_col, sy1, sx1 = load(piece, half, (1, 0), day_number, stack, validity)
    got1 = across(sy1)
    sy2, sx2, side = pl.pallas_call(
        second_kernel,
        in_specs=[VMEM] * 4,
        out_specs=[VMEM] * 3,
        out_shape=[packet] * 3,
        compiler_params=PARAMS,
        name="second",
    )(refl, valid, day_col, sx1)
    got2 = along(sy2)
    side = across(side)
    join = dict(
        in_specs=[VMEM] * 2, out_specs=VMEM, out_shape=packet, compiler_params=PARAMS
    )
    joined1 = pl.pallas_call(join_near_kernel, name="join_first", **join)(sy1, got1)
    far1 = along(joined1)
    joined2 = pl.pallas_call(join_own_kernel, name="join_second", **join)(sx2, got2)
    far2 = across(joined2)
    arrays = (refl, valid, day_col)
    out = fill("fill_first", 0, piece, merge_first, *arrays, (far1, side, got1))
    out = fill("fill_second", half, piece, merge_second, *arrays, (got2, far2, side), out)
    return jnp.transpose(out, (1, 0, 2))


def solution(mesh):
    placed = (P("date", None, ("tile", "pix")), P("date", ("tile", "pix")), P("date"))
    devices = mesh.shape["date"]
    return jax.shard_map(
        body if devices == 4 else functools.partial(body_any, devices),
        mesh=mesh,
        in_specs=placed,
        out_specs=P("date", None, ("tile", "pix")),
        check_vma=False,
    )
```

time: 108 us -> 17.8 us (0.16)
  blocking collectives: 42.2 us -> 0 us
  local copies, waits for them, and re-layouts: 35.1 us -> 0 us
  other arithmetic: 29.2 us -> 0 us
  starting transfers between devices: 0 us -> 9.57 us
  Pallas kernels: 0 us -> 5.07 us
  waiting for transfers between devices: 0 us -> 2.95 us
    all_gather x4 -> x0, blocking collectives: 42.2 us -> none  [the longest x1 12.3 us: body(): pb_val = lax.all_gather(bwd_val[:1], 'date', axis=0, tiled=True)]
    pad x16 -> x0, local copies, waits for them, and re-layouts: 14.9 us -> none  [the longest x8 9.27 us: scan_block(): lax.associative_scan(pass_forward, (jnp.where(live, day_col, -1), values)...]
    slice x16 -> x0, local copies, waits for them, and re-layouts: 12.6 us -> none  [the longest x9 8.14 us: scan_block(): lax.associative_scan(pass_backward, (jnp.where(live, day_col, far_day), v...]
    select_n x19 -> x0, other arithmetic: 10 us -> none  [the longest x1 3.67 us: blend(): return jnp.where(live[:, None, :], values, chosen)]
    ppermute x0 -> x5, starting transfers between devices: none -> 9.57 us  [the longest x3 5.35 us: body(): across = lambda x: lax.ppermute(x, 'date', [(d, d ^ 1) for d in range(4)])]
    add x12 -> x0, other arithmetic: 8.4 us -> none  [the longest x7 5.24 us: scan_block(): lax.associative_scan(pass_backward, (jnp.where(live, day_col, far_day), v...]
    pallas_call x0 -> x6, Pallas kernels: none -> 5.07 us  [the longest x2 2.74 us: fill(): pl.pallas_call(functools.partial(fill_kernel, start, width, piece, len(go...]
    unnamed x25 -> x0, local copies, waits for them, and re-layouts: 4.34 us -> none
  transfers between devices with their start and end apart: 0 -> 5, of which waited for: 0 -> 3; matrix products, arithmetic and copies ran while one was open for 0% -> 0% of each run, Pallas kernels for 0% -> 11%
where the time goes in v2:
time: 17.8 us; the launch traced here: 17.6 us
  starting transfers between devices  9.57 us (54%)
  Pallas kernels  5.07 us (28%)
  waiting for transfers between devices  2.95 us (17%)
    ppermute x3, starting transfers between devices, body(): across = lambda x: lax.ppermute(x, 'date', [(d, d ^ 1) for d in range(4)])  5.35 us
    ppermute x2, starting transfers between devices, body(): along = lambda x: lax.ppermute(x, 'date', [(d, d ^ 2) for d in range(4)])  4.22 us
    pallas_call x2, Pallas kernels, fill(): pl.pallas_call(functools.partial(fill_kernel, start, width, piece, len(go...  2.74 us
    ppermute x3, waiting for transfers between devices, body(): across = lambda x: lax.ppermute(x, 'date', [(d, d ^ 1) for d in range(4)])  1.89 us
    pallas_call x1, Pallas kernels, load(): pl.pallas_call(functools.partial(load_kernel, piece, bits), in_specs=[HBM...  1.76 us
    ppermute x2, waiting for transfers between devices, body(): along = lambda x: lax.ppermute(x, 'date', [(d, d ^ 2) for d in range(4)])  1.06 us
    pallas_call x1, Pallas kernels, body(): pl.pallas_call(second_kernel, in_specs=[VMEM] * 4, out_specs=[VMEM] * 3,...  0.4 us
  transfers between devices with their start and end apart: 5, of which 3 were waited for; matrix products, arithmetic and copies ran while one was open for 0% of the time, Pallas kernels for 11%

profile of v2, /device:TPU:0, one launch (start us, length us, event | category | flops | bytes accessed | tf_op | source)
XLA Modules:
  0.0 17.6 jit_solution(17936799127532877662)
XLA Ops:
  0.0 1.8 %load.1 = (f32[7,8,8192]{2,1,0:T(8,128)S(1)}, s32[8,8192]{1,0:T(8,128)S(1)}, f32[8,128]{1,0:T(8,128)S(1)}, f32[8,4096]{1,0:T(8,128)S(1)}, f32[8,4096]{1,0:T(8,128)S(1)}) custom-call(s32[8]{0:T(128)} %days_in.1, f32[7,8,8192]{2,1,0:T(8,128)} %bitcast.2, s32[8,8192]{1,0:T(8,128)} %valid_in.1), custom_call_target="tpu_custom_call" | custom-call | tf_op jit(solution)/shard_map/load/pallas_call | solution.py:280
  1.8 3.0 %collective-permute-start.3 = (f32[8,4096]{1,0:T(8,128)S(1)}, f32[8,4096]{1,0:T(8,128)S(1)}, u32[]{:S(2)}, u32[]{:S(2)}) collective-permute-start(f32[8,4096]{1,0:T(8,128)S(1)} %get-tuple-element.20.own), channel_id=1, source_target_pairs={{0,8},{8,0},{16,24},{24,16},{1,9},{9,1},{17,25},{25,17},{2,10},{10... | collective-permute-start | bytes 393224 | tf_op jit(solution)/shard_map/ppermute | solution.py:322
  4.8 0.4 %second.1 = (f32[8,4096]{1,0:T(8,128)S(1)}, f32[8,4096]{1,0:T(8,128)S(1)}, f32[8,4096]{1,0:T(8,128)S(1)}) custom-call(f32[7,8,8192]{2,1,0:T(8,128)S(1)} %get-tuple-element.13.refl, s32[8,8192]{1,0:T(8,128)S(1)} %get-tuple-element.14.valid, f32[8,128]{1,0:T(8,128)S(1)} %get-tuple-element.15.day_in, f32[8,4096]{1,0:T(8,128)S(1)} %get-tuple-element.16.sx_first), custom_call_target="tpu_custom_call" | custom-call | tf_op jit(solution)/shard_map/second/pallas_call | solution.py:327
  5.2 1.6 %collective-permute-start = (f32[8,4096]{1,0:T(8,128)S(1)}, f32[8,4096]{1,0:T(8,128)S(1)}, u32[]{:S(2)}, u32[]{:S(2)}) collective-permute-start(f32[8,4096]{1,0:T(8,128)S(1)} %get-tuple-element.17), channel_id=1, source_target_pairs={{0,16},{8,24},{16,0},{24,8},{1,17},{9,25},{17,1},{25,9},{2,18},{10... | collective-permute-start | bytes 393224 | tf_op jit(solution)/shard_map/ppermute | solution.py:323
  6.8 0.5 %collective-permute-start.2 = (f32[8,4096]{1,0:T(8,128)S(1)}, f32[8,4096]{1,0:T(8,128)S(1)}, u32[]{:S(2)}, u32[]{:S(2)}) collective-permute-start(f32[8,4096]{1,0:T(8,128)S(1)} %get-tuple-element.19), channel_id=1, source_target_pairs={{0,8},{8,0},{16,24},{24,16},{1,9},{9,1},{17,25},{25,17},{2,10},{10... | collective-permute-start | bytes 393224 | tf_op jit(solution)/shard_map/ppermute | solution.py:322
  7.3 1.1 %collective-permute-done.3.got.rest_2_ = f32[8,4096]{1,0:T(8,128)S(1)} collective-permute-done((f32[8,4096]{1,0:T(8,128)S(1)}, f32[8,4096]{1,0:T(8,128)S(1)}, u32[]{:S(2)}, u32[]{:S(2)}) %collective-permute-start.3) | collective-permute-done | bytes 131104 | tf_op jit(solution)/shard_map/ppermute | solution.py:322
  8.4 0.1 join_first.1
  8.5 2.6 %collective-permute-start.4 = (f32[8,4096]{1,0:T(8,128)S(1)}, f32[8,4096]{1,0:T(8,128)S(1)}, u32[]{:S(2)}, u32[]{:S(2)}) collective-permute-start(f32[8,4096]{1,0:T(8,128)S(1)} %join_first.1), channel_id=1, source_target_pairs={{0,16},{8,24},{16,0},{24,8},{1,17},{9,25},{17,1},{25,9},{2,18},{10... | collective-permute-start | bytes 393224 | tf_op jit(solution)/shard_map/ppermute | solution.py:323
  11.1 0.0 collective-permute-done.got.rest_0_
  11.1 0.1 join_second.1
  11.2 1.8 %collective-permute-start.1 = (f32[8,4096]{1,0:T(8,128)S(1)}, f32[8,4096]{1,0:T(8,128)S(1)}, u32[]{:S(2)}, u32[]{:S(2)}) collective-permute-start(f32[8,4096]{1,0:T(8,128)S(1)} %join_second.1), channel_id=1, source_target_pairs={{0,8},{8,0},{16,24},{24,16},{1,9},{9,1},{17,25},{25,17},{2,10},{10... | collective-permute-start | bytes 393224 | tf_op jit(solution)/shard_map/ppermute | solution.py:322
  13.0 0.0 collective-permute-done.2.rest_1_.rest_2_
  13.0 1.1 %collective-permute-done.4.rest_0_ = f32[8,4096]{1,0:T(8,128)S(1)} collective-permute-done((f32[8,4096]{1,0:T(8,128)S(1)}, f32[8,4096]{1,0:T(8,128)S(1)}, u32[]{:S(2)}, u32[]{:S(2)}) %collective-permute-start.4) | collective-permute-done | bytes 131104 | tf_op jit(solution)/shard_map/ppermute | solution.py:323
  14.1 1.4 %fill_first.1.rest_3_ = f32[7,8,8192]{2,1,0:T(8,128)} custom-call(f32[7,8,8192]{2,1,0:T(8,128)S(1)} %get-tuple-element.13.refl, s32[8,8192]{1,0:T(8,128)S(1)} %get-tuple-element.14.valid, f32[8,128]{1,0:T(8,128)S(1)} %get-tuple-element.15.day_in, f32[8,4096]{1,0:T(8,128)S(1)} %collective-permute-done.4.rest_0_, ...), custom_call_target="tpu_custom_call" | custom-call | tf_op jit(solution)/shard_map/fill_first/pallas_call | solution.py:262
  15.4 0.8 %collective-permute-done.1.rest_1_ = f32[8,4096]{1,0:T(8,128)S(1)} collective-permute-done((f32[8,4096]{1,0:T(8,128)S(1)}, f32[8,4096]{1,0:T(8,128)S(1)}, u32[]{:S(2)}, u32[]{:S(2)}) %collective-permute-start.1) | collective-permute-done | bytes 131104 | tf_op jit(solution)/shard_map/ppermute | solution.py:322
  16.3 1.4 %fill_second.1 = f32[7,8,8192]{2,1,0:T(8,128)} custom-call(f32[7,8,8192]{2,1,0:T(8,128)S(1)} %get-tuple-element.13.refl, s32[8,8192]{1,0:T(8,128)S(1)} %get-tuple-element.14.valid, f32[8,128]{1,0:T(8,128)S(1)} %get-tuple-element.15.day_in, f32[8,4096]{1,0:T(8,128)S(1)} %collective-permute-done.got.rest_0_, ...), custom_call_target="tpu_custom_call", output_to_operand_aliasing={{}: (6, {})} | custom-call | tf_op jit(solution)/shard_map/fill_second/pallas_call | solution.py:262
Async XLA Ops:
  1.8 6.6 %collective-permute-start.3 = (f32[8,4096]{1,0:T(8,128)S(1)}, f32[8,4096]{1,0:T(8,128)S(1)}, u32[]{:S(2)}, u32[]{:S(2)}) collective-permute-start(f32[8,4096]{1,0:T(8,128)S(1)} %get-tuple-element.20.own), channel_id=1, source_target_pairs={{0,8},{8,0},{16,24},{24,16},{1,9},{9,1},{17,25},{25,17},{2,10},{10... | collective-permute-start | bytes 393224 | tf_op jit(solution)/shard_map/ppermute | solution.py:322
  5.2 5.9 %collective-permute-start = (f32[8,4096]{1,0:T(8,128)S(1)}, f32[8,4096]{1,0:T(8,128)S(1)}, u32[]{:S(2)}, u32[]{:S(2)}) collective-permute-start(f32[8,4096]{1,0:T(8,128)S(1)} %get-tuple-element.17), channel_id=1, source_target_pairs={{0,16},{8,24},{16,0},{24,8},{1,17},{9,25},{17,1},{25,9},{2,18},{10... | collective-permute-start | bytes 393224 | tf_op jit(solution)/shard_map/ppermute | solution.py:323
  6.8 6.2 %collective-permute-start.2 = (f32[8,4096]{1,0:T(8,128)S(1)}, f32[8,4096]{1,0:T(8,128)S(1)}, u32[]{:S(2)}, u32[]{:S(2)}) collective-permute-start(f32[8,4096]{1,0:T(8,128)S(1)} %get-tuple-element.19), channel_id=1, source_target_pairs={{0,8},{8,0},{16,24},{24,16},{1,9},{9,1},{17,25},{25,17},{2,10},{10... | collective-permute-start | bytes 393224 | tf_op jit(solution)/shard_map/ppermute | solution.py:322
  8.5 5.6 %collective-permute-start.4 = (f32[8,4096]{1,0:T(8,128)S(1)}, f32[8,4096]{1,0:T(8,128)S(1)}, u32[]{:S(2)}, u32[]{:S(2)}) collective-permute-start(f32[8,4096]{1,0:T(8,128)S(1)} %join_first.1), channel_id=1, source_target_pairs={{0,16},{8,24},{16,0},{24,8},{1,17},{9,25},{17,1},{25,9},{2,18},{10... | collective-permute-start | bytes 393224 | tf_op jit(solution)/shard_map/ppermute | solution.py:323
  11.2 5.0 %collective-permute-start.1 = (f32[8,4096]{1,0:T(8,128)S(1)}, f32[8,4096]{1,0:T(8,128)S(1)}, u32[]{:S(2)}, u32[]{:S(2)}) collective-permute-start(f32[8,4096]{1,0:T(8,128)S(1)} %join_second.1), channel_id=1, source_target_pairs={{0,8},{8,0},{16,24},{24,16},{1,9},{9,1},{17,25},{25,17},{2,10},{10... | collective-permute-start | bytes 393224 | tf_op jit(solution)/shard_map/ppermute | solution.py:322

commit v3 on v2

--- a/solution.py
+++ b/solution.py
@@ -78,16 +78,16 @@
     return rows, packet_rows
 
 
-def load_kernel(piece, bits, days_in, refl_in, valid_in, refl, valid, day_out, *rest):
-    sends, (days, day_sem, sems) = rest[: len(bits)], rest[len(bits) :]
+def load_kernel(piece, bits, days_in, refl_in, valid_in, day_out, *rest):
+    sends, (refl, valid, days, day_sem, sems) = rest[: len(bits)], rest[len(bits) :]
     bands, count, pixels = refl.shape
     half = sends[0].shape[1]
     day_copy = pltpu.make_async_copy(days_in, days, day_sem)
     day_copy.start()
     copies = []
     at = 0
-    while at < pixels:
-        width = piece if at < half else pixels - half
+    while at < half:
+        width = piece
         cols = pl.ds(at, width)
         k = len(copies)
         pair = (
@@ -99,7 +99,7 @@
             ),
         )
         for c in pair:
-            c.start()
+            c.start(priority=1)
         copies.append(pair)
         at += width
     rows, packet_rows = tile_rows(bands, count)
@@ -124,12 +124,8 @@
                 for send, packet in zip(sends, packets):
                     send[:, cols] = packet
 
-    for pair in copies[half // piece :]:
-        for c in pair:
-            c.wait()
-
-
-def second_kernel(refl, valid, day_in, sx_first, sy, sx, side):
+
+def second_kernel(refl, valid, day_in, sy, sx, side):
     bands, count, pixels = refl.shape
     half = pixels // 2
     rows, packet_rows = tile_rows(bands, count)
@@ -146,7 +142,10 @@
             a, b = packet_of(values, live, day_col, rows, packet_rows, (upper, odd))
             sy[:, cols] = a
             sx[:, cols] = b
-            side[:, cols] = jnp.where(inner, sx_first[:, cols], b)
+            live = valid[:, cols] > 0
+            values = [refl[k, :, cols] for k in range(bands)]
+            (c,) = packet_of(values, live, day_col, rows, packet_rows, (odd,))
+            side[:, cols] = jnp.where(inner, c, b)
 
 
 def nearness(packet):
@@ -204,11 +203,35 @@
     return before, after
 
 
-def fill_kernel(start, width, piece, packets, merge, refl, valid, day_in, *rest):
-    gots = rest[:packets]
-    out, buf, sems = rest[-3:]
-    bands, count, _ = refl.shape
+def near_kernel(refl, valid, day_in, prev_out, next_out, prev_days, next_days):
+    bands, count, pixels = refl.shape
     rows, _ = tile_rows(bands, count)
+    day_col = day_in[...]
+
+    @pl.loop(0, pixels // LANES // 4)
+    def _(j):
+        for u in range(4):
+            cols = span_of(j * 4 + u)
+            live = valid[:, cols] > 0
+            prev_pos = running(jnp.where(live, rows, -1), rows, count, True)
+            next_pos = running(jnp.where(live, rows, count), rows, count, False)
+            prev_in = prev_pos >= 0
+            next_in = next_pos < count
+            prev_pos = prev_pos & (count - 1)
+            next_pos = next_pos & (count - 1)
+            prev_days[:, cols] = jnp.where(prev_in, pick(day_col, prev_pos), 0.0)
+            next_days[:, cols] = jnp.where(next_in, pick(day_col, next_pos), TOP)
+            for b in range(bands):
+                x = refl[b, :, cols]
+                prev_out[b, :, cols] = pick(x, prev_pos)
+                next_out[b, :, cols] = pick(x, next_pos)
+
+
+def fill_kernel(start, width, piece, packets, merge, *refs):
+    prev_own, next_own, prev_days, next_days, day_in = refs[:5]
+    gots = refs[5 : 5 + packets]
+    out, buf, sems = refs[-3:]
+    bands, count, _ = prev_own.shape
     day_col = day_in[...]
     copies = []
     for k in range(width // piece):
@@ -219,29 +242,20 @@
                 i = k * (piece // LANES) + j * 4 + u
                 cols = span_of(i)
                 far = span_of(start // LANES + i)
-                live = valid[:, far] > 0
-                prev_pos = running(jnp.where(live, rows, -1), rows, count, True)
-                next_pos = running(jnp.where(live, rows, count), rows, count, False)
-                prev_in = prev_pos >= 0
-                next_in = next_pos < count
-                prev_pos = prev_pos & (count - 1)
-                next_pos = next_pos & (count - 1)
                 before, after = merge(gots, cols)
-                prev_day = jnp.where(prev_in, pick(day_col, prev_pos), before[bands:])
-                next_day = jnp.where(
-                    next_in, pick(day_col, next_pos), TOP - after[bands:]
-                )
+                prev_day, next_day = prev_days[:, far], next_days[:, far]
+                prev_in, next_in = prev_day > 0.0, next_day < TOP
+                prev_day = jnp.where(prev_in, prev_day, before[bands:])
+                next_day = jnp.where(next_in, next_day, TOP - after[bands:])
                 has_prev = prev_day > 0.0
-                has_next = next_day < TOP
-                both = jnp.logical_and(has_prev, has_next)
+                both = jnp.logical_and(has_prev, next_day < TOP)
                 span = jnp.maximum(jnp.where(both, next_day - prev_day, 1.0), 1.0)
                 weight = jnp.where(
                     both, (day_col - prev_day) / span, jnp.where(has_prev, 0.0, 1.0)
                 )
                 for b in range(bands):
-                    x = refl[b, :, far]
-                    prev = jnp.where(prev_in, pick(x, prev_pos), before[b : b + 1])
-                    nxt = jnp.where(next_in, pick(x, next_pos), after[b : b + 1])
+                    prev = jnp.where(prev_in, prev_own[b, :, far], before[b : b + 1])
+                    nxt = jnp.where(next_in, next_own[b, :, far], after[b : b + 1])
                     buf[b, :, cols] = prev + weight * (nxt - prev)
 
         copy = pltpu.make_async_copy(
@@ -255,23 +269,35 @@
         copy.wait()
 
 
-def fill(name, start, piece, merge, refl, valid, day_col, gots, out=None):
+def nearest(refl, valid, day_col):
     bands, count, pixels = refl.shape
+    return pl.pallas_call(
+        near_kernel,
+        in_specs=[VMEM] * 3,
+        out_specs=[VMEM] * 4,
+        out_shape=[f32(bands, count, pixels)] * 2 + [f32(count, pixels)] * 2,
+        compiler_params=PARAMS,
+        name="nearest",
+    )(refl, valid, day_col)
+
+
+def fill(name, start, piece, merge, near, day_col, gots, out=None):
+    bands, count, pixels = near[0].shape
     width = gots[0].shape[1]
     held = () if out is None else (out,)
     return pl.pallas_call(
         functools.partial(fill_kernel, start, width, piece, len(gots), merge),
-        in_specs=[VMEM] * (3 + len(gots)) + [HBM] * len(held),
+        in_specs=[VMEM] * (5 + len(gots)) + [HBM] * len(held),
         out_specs=HBM,
         out_shape=f32(bands, count, pixels),
-        input_output_aliases={} if out is None else {3 + len(gots): 0},
+        input_output_aliases={} if out is None else {5 + len(gots): 0},
         scratch_shapes=[
             pltpu.VMEM((bands, count, width), jnp.float32),
             pltpu.SemaphoreType.DMA((width // piece,)),
         ],
         compiler_params=PARAMS,
         name=name,
-    )(refl, valid, day_col, *gots, *held)
+    )(*near, day_col, *gots, *held)
 
 
 def load(piece, width, bits, days, stack, validity):
@@ -280,14 +306,11 @@
     return pl.pallas_call(
         functools.partial(load_kernel, piece, bits),
         in_specs=[HBM] * 3,
-        out_specs=[VMEM] * (3 + len(bits)),
-        out_shape=[
-            f32(bands, count, pixels),
-            jax.ShapeDtypeStruct((count, pixels), jnp.int32),
-            f32(count, LANES),
-        ]
-        + [f32(bands + 1, width)] * len(bits),
+        out_specs=[VMEM] * (1 + len(bits)),
+        out_shape=[f32(count, LANES)] + [f32(bands + 1, width)] * len(bits),
         scratch_shapes=[
+            pltpu.VMEM((bands, count, width), jnp.float32),
+            pltpu.VMEM((count, width), jnp.int32),
             pltpu.SMEM((count,), jnp.int32),
             pltpu.SemaphoreType.DMA,
             pltpu.SemaphoreType.DMA((2 * (width // piece + 1),)),
@@ -302,14 +325,15 @@
     piece = pixels // 8
     stack = jnp.transpose(reflectance, (1, 0, 2))
     bits = list(range((devices - 1).bit_length()))
-    refl, valid, day_col, *sends = load(piece, pixels, bits, day_number, stack, validity)
+    day_col, *sends = load(piece, pixels, bits, day_number, stack, validity)
+    refl, valid = stack, validity
     gots, tops = [], []
     for k in range(1, 1 << len(bits)):
         pairs = [(d, d ^ k) for d in range(devices) if d ^ k < devices]
         tops.append(k.bit_length() - 1)
         gots.append(lax.ppermute(sends[tops[-1]], "date", pairs))
     merge = functools.partial(merge_all, tops)
-    out = fill("fill", 0, piece, merge, refl, valid, day_col, gots)
+    out = fill("fill", 0, piece, merge, nearest(refl, valid, day_col), day_col, gots)
     return jnp.transpose(out, (1, 0, 2))
 
 
@@ -322,16 +346,17 @@
     across = lambda x: lax.ppermute(x, "date", [(d, d ^ 1) for d in range(4)])
     along = lambda x: lax.ppermute(x, "date", [(d, d ^ 2) for d in range(4)])
 
-    refl, valid, day_col, sy1, sx1 = load(piece, half, (1, 0), day_number, stack, validity)
+    day_col, sy1 = load(piece, half, (1,), day_number, stack, validity)
+    refl, valid = stack, validity
     got1 = across(sy1)
     sy2, sx2, side = pl.pallas_call(
         second_kernel,
-        in_specs=[VMEM] * 4,
+        in_specs=[VMEM] * 3,
         out_specs=[VMEM] * 3,
         out_shape=[packet] * 3,
         compiler_params=PARAMS,
         name="second",
-    )(refl, valid, day_col, sx1)
+    )(refl, valid, day_col)
     got2 = along(sy2)
     side = across(side)
     join = dict(
@@ -341,7 +366,7 @@
     far1 = along(joined1)
     joined2 = pl.pallas_call(join_own_kernel, name="join_second", **join)(sx2, got2)
     far2 = across(joined2)
-    arrays = (refl, valid, day_col)
+    arrays = (nearest(refl, valid, day_col), day_col)
     out = fill("fill_first", 0, piece, merge_first, *arrays, (far1, side, got1))
     out = fill("fill_second", half, piece, merge_second, *arrays, (got2, far2, side), out)
     return jnp.transpose(out, (1, 0, 2))

time: 17.8 us -> 17.3 us (0.972)
  waiting for transfers between devices: 2.95 us -> 1.88 us
  Pallas kernels: 5.07 us -> 5.55 us
    ppermute x2, waiting for transfers between devices: 1.06 us -> 0.13 us  [body(): along = lambda x: lax.ppermute(x, 'date', [(d, d ^ 2) for d in range(4)])]
    pallas_call x1 -> x2, Pallas kernels: 0.4 us -> 1.31 us  [the longest x1 0.75 us: nearest(): pl.pallas_call(near_kernel, in_specs=[VMEM] * 3, out_specs=[VMEM] * 4, ou...]
    pallas_call x2, Pallas kernels: 2.74 us -> 2.48 us  [fill(): pl.pallas_call(functools.partial(fill_kernel, start, width, piece, len(go...]
  transfers between devices with their start and end apart: 5 -> 5, of which waited for: 3 -> 3; matrix products, arithmetic and copies ran while one was open for 0% -> 0% of each run, Pallas kernels for 11% -> 16%
where the time goes in v3:
time: 17.3 us; the launch traced here: 17.2 us
  starting transfers between devices  9.67 us (56%)
  Pallas kernels  5.55 us (32%)
  waiting for transfers between devices  1.88 us (11%)
    ppermute x3, starting transfers between devices, body(): across = lambda x: lax.ppermute(x, 'date', [(d, d ^ 1) for d in range(4)])  5.52 us
    ppermute x2, starting transfers between devices, body(): along = lambda x: lax.ppermute(x, 'date', [(d, d ^ 2) for d in range(4)])  4.15 us
    pallas_call x2, Pallas kernels, fill(): pl.pallas_call(functools.partial(fill_kernel, start, width, piece, len(go...  2.48 us
    ppermute x3, waiting for transfers between devices, body(): across = lambda x: lax.ppermute(x, 'date', [(d, d ^ 1) for d in range(4)])  1.75 us
    pallas_call x1, Pallas kernels, load(): pl.pallas_call(functools.partial(load_kernel, piece, bits), in_specs=[HBM...  1.58 us
    pallas_call x1, Pallas kernels, nearest(): pl.pallas_call(near_kernel, in_specs=[VMEM] * 3, out_specs=[VMEM] * 4, ou...  0.75 us
    pallas_call x1, Pallas kernels, body(): pl.pallas_call(second_kernel, in_specs=[VMEM] * 3, out_specs=[VMEM] * 3,...  0.55 us
  transfers between devices with their start and end apart: 5, of which 3 were waited for; matrix products, arithmetic and copies ran while one was open for 0% of the time, Pallas kernels for 16%

profile of v3, /device:TPU:0, one launch (start us, length us, event | category | flops | bytes accessed | tf_op | source)
XLA Modules:
  0.0 17.2 jit_solution(13286985526939049564)
XLA Ops:
  0.0 0.0 copy-start.1
  0.0 0.0 copy-start
  0.0 1.6 %load.1 = (f32[8,128]{1,0:T(8,128)S(1)}, f32[8,4096]{1,0:T(8,128)S(1)}) custom-call(s32[8]{0:T(128)} %days_in.1, f32[7,8,8192]{2,1,0:T(8,128)} %bitcast.2, s32[8,8192]{1,0:T(8,128)} %valid.3), custom_call_target="tpu_custom_call" | custom-call | tf_op jit(solution)/shard_map/load/pallas_call | solution.py:306
  1.6 3.0 %collective-permute-start.3 = (f32[8,4096]{1,0:T(8,128)S(1)}, f32[8,4096]{1,0:T(8,128)S(1)}, u32[]{:S(2)}, u32[]{:S(2)}) collective-permute-start(f32[8,4096]{1,0:T(8,128)S(1)} %get-tuple-element.22.own), channel_id=1, source_target_pairs={{0,8},{8,0},{16,24},{24,16},{1,9},{9,1},{17,25},{25,17},{2,10},{10... | collective-permute-start | bytes 393224 | tf_op jit(solution)/shard_map/ppermute | solution.py:346
  4.6 0.0 copy-done.1
  4.6 0.0 copy-done
  4.6 0.6 %second.1 = (f32[8,4096]{1,0:T(8,128)S(1)}, f32[8,4096]{1,0:T(8,128)S(1)}, f32[8,4096]{1,0:T(8,128)S(1)}) custom-call(f32[7,8,8192]{2,1,0:T(8,128)S(1)} %bitcast.3, s32[8,8192]{1,0:T(8,128)S(1)} %copy-done.1, f32[8,128]{1,0:T(8,128)S(1)} %get-tuple-element.14.day_in.refs_4_), custom_call_target="tpu_custom_call" | custom-call | tf_op jit(solution)/shard_map/second/pallas_call | solution.py:352
  5.2 1.6 %collective-permute-start = (f32[8,4096]{1,0:T(8,128)S(1)}, f32[8,4096]{1,0:T(8,128)S(1)}, u32[]{:S(2)}, u32[]{:S(2)}) collective-permute-start(f32[8,4096]{1,0:T(8,128)S(1)} %get-tuple-element.19), channel_id=1, source_target_pairs={{0,16},{8,24},{16,0},{24,8},{1,17},{9,25},{17,1},{25,9},{2,18},{10... | collective-permute-start | bytes 393224 | tf_op jit(solution)/shard_map/ppermute | solution.py:347
  6.8 0.5 %collective-permute-start.2 = (f32[8,4096]{1,0:T(8,128)S(1)}, f32[8,4096]{1,0:T(8,128)S(1)}, u32[]{:S(2)}, u32[]{:S(2)}) collective-permute-start(f32[8,4096]{1,0:T(8,128)S(1)} %get-tuple-element.21), channel_id=1, source_target_pairs={{0,8},{8,0},{16,24},{24,16},{1,9},{9,1},{17,25},{25,17},{2,10},{10... | collective-permute-start | bytes 393224 | tf_op jit(solution)/shard_map/ppermute | solution.py:346
  7.3 0.8 %collective-permute-done.3.got.refs_7_ = f32[8,4096]{1,0:T(8,128)S(1)} collective-permute-done((f32[8,4096]{1,0:T(8,128)S(1)}, f32[8,4096]{1,0:T(8,128)S(1)}, u32[]{:S(2)}, u32[]{:S(2)}) %collective-permute-start.3) | collective-permute-done | bytes 131104 | tf_op jit(solution)/shard_map/ppermute | solution.py:346
  8.1 0.1 join_first.1
  8.2 2.6 %collective-permute-start.4 = (f32[8,4096]{1,0:T(8,128)S(1)}, f32[8,4096]{1,0:T(8,128)S(1)}, u32[]{:S(2)}, u32[]{:S(2)}) collective-permute-start(f32[8,4096]{1,0:T(8,128)S(1)} %join_first.1), channel_id=1, source_target_pairs={{0,16},{8,24},{16,0},{24,8},{1,17},{9,25},{17,1},{25,9},{2,18},{10... | collective-permute-start | bytes 393224 | tf_op jit(solution)/shard_map/ppermute | solution.py:347
  10.8 0.0 collective-permute-done.got.refs_5_
  10.8 0.1 join_second.1
  10.9 2.0 %collective-permute-start.1 = (f32[8,4096]{1,0:T(8,128)S(1)}, f32[8,4096]{1,0:T(8,128)S(1)}, u32[]{:S(2)}, u32[]{:S(2)}) collective-permute-start(f32[8,4096]{1,0:T(8,128)S(1)} %join_second.1), channel_id=1, source_target_pairs={{0,8},{8,0},{16,24},{24,16},{1,9},{9,1},{17,25},{25,17},{2,10},{10... | collective-permute-start | bytes 393224 | tf_op jit(solution)/shard_map/ppermute | solution.py:346
  12.8 0.8 %nearest.1 = (f32[7,8,8192]{2,1,0:T(8,128)S(1)}, f32[7,8,8192]{2,1,0:T(8,128)S(1)}, f32[8,8192]{1,0:T(8,128)S(1)}, f32[8,8192]{1,0:T(8,128)S(1)}) custom-call(f32[7,8,8192]{2,1,0:T(8,128)S(1)} %bitcast.4, s32[8,8192]{1,0:T(8,128)S(1)} %copy-done.1, f32[8,128]{1,0:T(8,128)S(1)} %get-tuple-element.14.day_in.refs_4_), custom_call_target="tpu_custom_call" | custom-call | tf_op jit(solution)/shard_map/nearest/pallas_call | solution.py:274
  13.6 0.0 collective-permute-done.2.refs_6_.refs_7_
  13.6 0.1 collective-permute-done.4.refs_5_
  13.7 1.2 %fill_first.1.refs_8_ = f32[7,8,8192]{2,1,0:T(8,128)} custom-call(f32[7,8,8192]{2,1,0:T(8,128)S(1)} %get-tuple-element.15.refs_0_, f32[7,8,8192]{2,1,0:T(8,128)S(1)} %get-tuple-element.16.refs_1_, f32[8,8192]{1,0:T(8,128)S(1)} %get-tuple-element.17.refs_2_, f32[8,8192]{1,0:T(8,128)S(1)} %get-tuple-element.18.refs_3_, ...), custom_call_target="tpu_custom_call" | custom-call | tf_op jit(solution)/shard_map/fill_first/pallas_call | solution.py:288
  15.0 0.9 %collective-permute-done.1.refs_6_ = f32[8,4096]{1,0:T(8,128)S(1)} collective-permute-done((f32[8,4096]{1,0:T(8,128)S(1)}, f32[8,4096]{1,0:T(8,128)S(1)}, u32[]{:S(2)}, u32[]{:S(2)}) %collective-permute-start.1) | collective-permute-done | bytes 131104 | tf_op jit(solution)/shard_map/ppermute | solution.py:346
  15.9 1.2 %fill_second.1 = f32[7,8,8192]{2,1,0:T(8,128)} custom-call(f32[7,8,8192]{2,1,0:T(8,128)S(1)} %get-tuple-element.15.refs_0_, f32[7,8,8192]{2,1,0:T(8,128)S(1)} %get-tuple-element.16.refs_1_, f32[8,8192]{1,0:T(8,128)S(1)} %get-tuple-element.17.refs_2_, f32[8,8192]{1,0:T(8,128)S(1)} %get-tuple-element.18.refs_3_, ...), custom_call_target="tpu_custom_call", output_to_operand_aliasing={{}: (8, {})} | custom-call | tf_op jit(solution)/shard_map/fill_second/pallas_call | solution.py:288
Async XLA Ops:
  0.0 4.6 %copy-start.1 = (s32[8,8192]{1,0:T(8,128)S(1)}, s32[8,8192]{1,0:T(8,128)}, u32[]{:S(2)}) copy-start(s32[8,8192]{1,0:T(8,128)} %valid.3) | copy-start | bytes 786436
  0.0 4.6 %copy-start = (f32[8,7,8192]{2,0,1:T(8,128)S(1)}, f32[8,7,8192]{2,0,1:T(8,128)}, u32[]{:S(2)}) copy-start(f32[8,7,8192]{2,0,1:T(8,128)} %param.3) | copy-start | bytes 5505028
  1.6 6.5 %collective-permute-start.3 = (f32[8,4096]{1,0:T(8,128)S(1)}, f32[8,4096]{1,0:T(8,128)S(1)}, u32[]{:S(2)}, u32[]{:S(2)}) collective-permute-start(f32[8,4096]{1,0:T(8,128)S(1)} %get-tuple-element.22.own), channel_id=1, source_target_pairs={{0,8},{8,0},{16,24},{24,16},{1,9},{9,1},{17,25},{25,17},{2,10},{10... | collective-permute-start | bytes 393224 | tf_op jit(solution)/shard_map/ppermute | solution.py:346
  5.2 5.6 %collective-permute-start = (f32[8,4096]{1,0:T(8,128)S(1)}, f32[8,4096]{1,0:T(8,128)S(1)}, u32[]{:S(2)}, u32[]{:S(2)}) collective-permute-start(f32[8,4096]{1,0:T(8,128)S(1)} %get-tuple-element.19), channel_id=1, source_target_pairs={{0,16},{8,24},{16,0},{24,8},{1,17},{9,25},{17,1},{25,9},{2,18},{10... | collective-permute-start | bytes 393224 | tf_op jit(solution)/shard_map/ppermute | solution.py:347
  6.8 6.8 %collective-permute-start.2 = (f32[8,4096]{1,0:T(8,128)S(1)}, f32[8,4096]{1,0:T(8,128)S(1)}, u32[]{:S(2)}, u32[]{:S(2)}) collective-permute-start(f32[8,4096]{1,0:T(8,128)S(1)} %get-tuple-element.21), channel_id=1, source_target_pairs={{0,8},{8,0},{16,24},{24,16},{1,9},{9,1},{17,25},{25,17},{2,10},{10... | collective-permute-start | bytes 393224 | tf_op jit(solution)/shard_map/ppermute | solution.py:346
  8.2 5.5 %collective-permute-start.4 = (f32[8,4096]{1,0:T(8,128)S(1)}, f32[8,4096]{1,0:T(8,128)S(1)}, u32[]{:S(2)}, u32[]{:S(2)}) collective-permute-start(f32[8,4096]{1,0:T(8,128)S(1)} %join_first.1), channel_id=1, source_target_pairs={{0,16},{8,24},{16,0},{24,8},{1,17},{9,25},{17,1},{25,9},{2,18},{10... | collective-permute-start | bytes 393224 | tf_op jit(solution)/shard_map/ppermute | solution.py:347
  10.9 5.0 %collective-permute-start.1 = (f32[8,4096]{1,0:T(8,128)S(1)}, f32[8,4096]{1,0:T(8,128)S(1)}, u32[]{:S(2)}, u32[]{:S(2)}) collective-permute-start(f32[8,4096]{1,0:T(8,128)S(1)} %join_second.1), channel_id=1, source_target_pairs={{0,8},{8,0},{16,24},{24,16},{1,9},{9,1},{17,25},{25,17},{2,10},{10... | collective-permute-start | bytes 393224 | tf_op jit(solution)/shard_map/ppermute | solution.py:346

commit v4 on v3

--- a/solution.py
+++ b/solution.py
@@ -6,6 +6,7 @@
 from jax.experimental import pallas as pl
 from jax.experimental.pallas import tpu as pltpu
 from jax.sharding import PartitionSpec as P
+
 
 LANES = 128
 TOP = 1048576.0
@@ -80,7 +81,7 @@
 
 def load_kernel(piece, bits, days_in, refl_in, valid_in, day_out, *rest):
     sends, (refl, valid, days, day_sem, sems) = rest[: len(bits)], rest[len(bits) :]
-    bands, count, pixels = refl.shape
+    bands, count, _ = refl.shape
     half = sends[0].shape[1]
     day_copy = pltpu.make_async_copy(days_in, days, day_sem)
     day_copy.start()
@@ -125,11 +126,11 @@
                     send[:, cols] = packet
 
 
-def second_kernel(refl, valid, day_in, sy, sx, side):
+def second_kernel(refl, valid, day_in, sy):
     bands, count, pixels = refl.shape
     half = pixels // 2
     rows, packet_rows = tile_rows(bands, count)
-    odd, upper, inner = flags()
+    _, upper, _ = flags()
     day_col = day_in[...]
 
     @pl.loop(0, half // LANES // 4)
@@ -138,9 +139,26 @@
             cols = span_of(j * 4 + u)
             far = span_of(half // LANES + j * 4 + u)
             live = valid[:, far] > 0
-            values = [refl[b, :, far] for b in range(bands)]
-            a, b = packet_of(values, live, day_col, rows, packet_rows, (upper, odd))
+            values = [refl[k, :, far] for k in range(bands)]
+            (a,) = packet_of(values, live, day_col, rows, packet_rows, (upper,))
             sy[:, cols] = a
+
+
+def side_kernel(refl, valid, day_in, sx, side):
+    bands, count, pixels = refl.shape
+    half = pixels // 2
+    rows, packet_rows = tile_rows(bands, count)
+    odd, _, inner = flags()
+    day_col = day_in[...]
+
+    @pl.loop(0, half // LANES // 4)
+    def _(j):
+        for u in range(4):
+            cols = span_of(j * 4 + u)
+            far = span_of(half // LANES + j * 4 + u)
+            live = valid[:, far] > 0
+            values = [refl[k, :, far] for k in range(bands)]
+            (b,) = packet_of(values, live, day_col, rows, packet_rows, (odd,))
             sx[:, cols] = b
             live = valid[:, cols] > 0
             values = [refl[k, :, cols] for k in range(bands)]
@@ -231,7 +249,7 @@
     prev_own, next_own, prev_days, next_days, day_in = refs[:5]
     gots = refs[5 : 5 + packets]
     out, buf, sems = refs[-3:]
-    bands, count, _ = prev_own.shape
+    bands, _, _ = prev_own.shape
     day_col = day_in[...]
     copies = []
     for k in range(width // piece):
@@ -281,7 +299,7 @@
     )(refl, valid, day_col)
 
 
-def fill(name, start, piece, merge, near, day_col, gots, out=None):
+def fill(start, piece, merge, near, day_col, gots, out=None):
     bands, count, pixels = near[0].shape
     width = gots[0].shape[1]
     held = () if out is None else (out,)
@@ -296,12 +314,11 @@
             pltpu.SemaphoreType.DMA((width // piece,)),
         ],
         compiler_params=PARAMS,
-        name=name,
     )(*near, day_col, *gots, *held)
 
 
 def load(piece, width, bits, days, stack, validity):
-    bands, count, pixels = stack.shape
+    bands, count, _ = stack.shape
     args = (pltpu.with_memory_space_constraint(a, pltpu.HBM) for a in (days, stack, validity))
     return pl.pallas_call(
         functools.partial(load_kernel, piece, bits),
@@ -333,31 +350,39 @@
         tops.append(k.bit_length() - 1)
         gots.append(lax.ppermute(sends[tops[-1]], "date", pairs))
     merge = functools.partial(merge_all, tops)
-    out = fill("fill", 0, piece, merge, nearest(refl, valid, day_col), day_col, gots)
+    out = fill(0, piece, merge, nearest(refl, valid, day_col), day_col, gots)
     return jnp.transpose(out, (1, 0, 2))
 
 
 def body(reflectance, validity, day_number):
-    count, bands, pixels = reflectance.shape
+    _, bands, pixels = reflectance.shape
     half = pixels // 2
     piece = half // 4
     stack = jnp.transpose(reflectance, (1, 0, 2))
     packet = f32(bands + 1, half)
-    across = lambda x: lax.ppermute(x, "date", [(d, d ^ 1) for d in range(4)])
-    along = lambda x: lax.ppermute(x, "date", [(d, d ^ 2) for d in range(4)])
+
+    def across(x):
+        return lax.ppermute(x, "date", [(d, d ^ 1) for d in range(4)])
+
+    def along(x):
+        return lax.ppermute(x, "date", [(d, d ^ 2) for d in range(4)])
 
     day_col, sy1 = load(piece, half, (1,), day_number, stack, validity)
     refl, valid = stack, validity
     got1 = across(sy1)
-    sy2, sx2, side = pl.pallas_call(
-        second_kernel,
-        in_specs=[VMEM] * 3,
-        out_specs=[VMEM] * 3,
-        out_shape=[packet] * 3,
-        compiler_params=PARAMS,
-        name="second",
-    )(refl, valid, day_col)
+
+    def packets(kernel, results):
+        return pl.pallas_call(
+            kernel,
+            in_specs=[VMEM] * 3,
+            out_specs=[VMEM] * results,
+            out_shape=[packet] * results,
+            compiler_params=PARAMS,
+        )(refl, valid, day_col)
+
+    (sy2,) = packets(second_kernel, 1)
     got2 = along(sy2)
+    sx2, side = packets(side_kernel, 2)
     side = across(side)
     join = dict(
         in_specs=[VMEM] * 2, out_specs=VMEM, out_shape=packet, compiler_params=PARAMS
@@ -367,8 +392,8 @@
     joined2 = pl.pallas_call(join_own_kernel, name="join_second", **join)(sx2, got2)
     far2 = across(joined2)
     arrays = (nearest(refl, valid, day_col), day_col)
-    out = fill("fill_first", 0, piece, merge_first, *arrays, (far1, side, got1))
-    out = fill("fill_second", half, piece, merge_second, *arrays, (got2, far2, side), out)
+    out = fill(0, piece, merge_first, *arrays, (far1, side, got1))
+    out = fill(half, piece, merge_second, *arrays, (got2, far2, side), out)
     return jnp.transpose(out, (1, 0, 2))
 
 

time: 17.3 us -> 17.2 us (level)
  waiting for transfers between devices: 1.88 us -> 1.54 us
    ppermute x5, waiting for transfers between devices: 1.88 us -> 1.54 us  [the longest x3 1.54 us: across(): return lax.ppermute(x, 'date', [(d, d ^ 1) for d in range(4)])]
    pallas_call x1 -> x2, Pallas kernels: 0.55 us -> 0.67 us  [packets(): pl.pallas_call(kernel, in_specs=[VMEM] * 3, out_specs=[VMEM] * results, o...]
  transfers between devices with their start and end apart: 5 -> 5, of which waited for: 3 -> 2; matrix products, arithmetic and copies ran while one was open for 0% -> 0% of each run, Pallas kernels for 16% -> 17%
where the time goes in v4:
time: 17.2 us; the launch traced here: 17 us
  starting transfers between devices  9.74 us (57%)
  Pallas kernels  5.67 us (33%)
  waiting for transfers between devices  1.54 us (9%)
    ppermute x3, starting transfers between devices, across(): return lax.ppermute(x, 'date', [(d, d ^ 1) for d in range(4)])  5.77 us
    ppermute x2, starting transfers between devices, along(): return lax.ppermute(x, 'date', [(d, d ^ 2) for d in range(4)])  3.97 us
    pallas_call x2, Pallas kernels, fill(): pl.pallas_call(functools.partial(fill_kernel, start, width, piece, len(go...  2.49 us
    pallas_call x1, Pallas kernels, load(): pl.pallas_call(functools.partial(load_kernel, piece, bits), in_specs=[HBM...  1.58 us
    ppermute x3, waiting for transfers between devices, across(): return lax.ppermute(x, 'date', [(d, d ^ 1) for d in range(4)])  1.54 us
    pallas_call x1, Pallas kernels, nearest(): pl.pallas_call(near_kernel, in_specs=[VMEM] * 3, out_specs=[VMEM] * 4, ou...  0.75 us
    pallas_call x2, Pallas kernels, packets(): pl.pallas_call(kernel, in_specs=[VMEM] * 3, out_specs=[VMEM] * results, o...  0.67 us
  transfers between devices with their start and end apart: 5, of which 2 were waited for; matrix products, arithmetic and copies ran while one was open for 0% of the time, Pallas kernels for 17%

profile of v4, /device:TPU:0, one launch (start us, length us, event | category | flops | bytes accessed | tf_op | source)
XLA Modules:
  0.0 17.0 jit_solution(2385433681033385930)
XLA Ops:
  0.0 0.0 copy-start.1
  0.0 0.0 copy-start
  0.0 1.6 %load.1 = (f32[8,128]{1,0:T(8,128)S(1)}, f32[8,4096]{1,0:T(8,128)S(1)}) custom-call(s32[8]{0:T(128)} %days_in.1, f32[7,8,8192]{2,1,0:T(8,128)} %bitcast.2, s32[8,8192]{1,0:T(8,128)} %valid.5), custom_call_target="tpu_custom_call" | custom-call | tf_op jit(solution)/shard_map/load/pallas_call | solution.py:323
  1.6 3.0 %collective-permute-start.3 = (f32[8,4096]{1,0:T(8,128)S(1)}, f32[8,4096]{1,0:T(8,128)S(1)}, u32[]{:S(2)}, u32[]{:S(2)}) collective-permute-start(f32[8,4096]{1,0:T(8,128)S(1)} %get-tuple-element.20.own), channel_id=1, source_target_pairs={{0,8},{8,0},{16,24},{24,16},{1,9},{9,1},{17,25},{25,17},{2,10},{10... | collective-permute-start | bytes 393224 | tf_op jit(solution)/shard_map/ppermute | solution.py:365
  4.6 0.0 copy-done.1
  4.6 0.0 copy-done
  4.6 0.3 %shard_map.37 = f32[8,4096]{1,0:T(8,128)S(1)} custom-call(f32[7,8,8192]{2,1,0:T(8,128)S(1)} %bitcast.3, s32[8,8192]{1,0:T(8,128)S(1)} %copy-done.1, f32[8,128]{1,0:T(8,128)S(1)} %get-tuple-element.13.day_in.refs_4_), custom_call_target="tpu_custom_call" | custom-call | tf_op jit(solution)/shard_map/pallas_call | solution.py:375
  4.9 1.6 %collective-permute-start = (f32[8,4096]{1,0:T(8,128)S(1)}, f32[8,4096]{1,0:T(8,128)S(1)}, u32[]{:S(2)}, u32[]{:S(2)}) collective-permute-start(f32[8,4096]{1,0:T(8,128)S(1)} %shard_map.37), channel_id=1, source_target_pairs={{0,16},{8,24},{16,0},{24,8},{1,17},{9,25},{17,1},{25,9},{2,18},{10... | collective-permute-start | bytes 393224 | tf_op jit(solution)/shard_map/ppermute | solution.py:368
  6.5 0.4 %shard_map.38 = (f32[8,4096]{1,0:T(8,128)S(1)}, f32[8,4096]{1,0:T(8,128)S(1)}) custom-call(f32[7,8,8192]{2,1,0:T(8,128)S(1)} %bitcast.4, s32[8,8192]{1,0:T(8,128)S(1)} %copy-done.1, f32[8,128]{1,0:T(8,128)S(1)} %get-tuple-element.13.day_in.refs_4_), custom_call_target="tpu_custom_call" | custom-call | tf_op jit(solution)/shard_map/pallas_call | solution.py:375
  6.9 0.6 %collective-permute-start.2 = (f32[8,4096]{1,0:T(8,128)S(1)}, f32[8,4096]{1,0:T(8,128)S(1)}, u32[]{:S(2)}, u32[]{:S(2)}) collective-permute-start(f32[8,4096]{1,0:T(8,128)S(1)} %get-tuple-element.19), channel_id=1, source_target_pairs={{0,8},{8,0},{16,24},{24,16},{1,9},{9,1},{17,25},{25,17},{2,10},{10... | collective-permute-start | bytes 393224 | tf_op jit(solution)/shard_map/ppermute | solution.py:365
  7.5 0.6 %collective-permute-done.3.got.refs_7_ = f32[8,4096]{1,0:T(8,128)S(1)} collective-permute-done((f32[8,4096]{1,0:T(8,128)S(1)}, f32[8,4096]{1,0:T(8,128)S(1)}, u32[]{:S(2)}, u32[]{:S(2)}) %collective-permute-start.3) | collective-permute-done | bytes 131104 | tf_op jit(solution)/shard_map/ppermute | solution.py:365
  8.1 0.1 join_first.1
  8.2 2.4 %collective-permute-start.4 = (f32[8,4096]{1,0:T(8,128)S(1)}, f32[8,4096]{1,0:T(8,128)S(1)}, u32[]{:S(2)}, u32[]{:S(2)}) collective-permute-start(f32[8,4096]{1,0:T(8,128)S(1)} %join_first.1), channel_id=1, source_target_pairs={{0,16},{8,24},{16,0},{24,8},{1,17},{9,25},{17,1},{25,9},{2,18},{10... | collective-permute-start | bytes 393224 | tf_op jit(solution)/shard_map/ppermute | solution.py:368
  10.6 0.0 collective-permute-done.got.refs_5_
  10.6 0.1 join_second.1
  10.7 2.1 %collective-permute-start.1 = (f32[8,4096]{1,0:T(8,128)S(1)}, f32[8,4096]{1,0:T(8,128)S(1)}, u32[]{:S(2)}, u32[]{:S(2)}) collective-permute-start(f32[8,4096]{1,0:T(8,128)S(1)} %join_second.1), channel_id=1, source_target_pairs={{0,8},{8,0},{16,24},{24,16},{1,9},{9,1},{17,25},{25,17},{2,10},{10... | collective-permute-start | bytes 393224 | tf_op jit(solution)/shard_map/ppermute | solution.py:365
  12.8 0.8 %nearest.1 = (f32[7,8,8192]{2,1,0:T(8,128)S(1)}, f32[7,8,8192]{2,1,0:T(8,128)S(1)}, f32[8,8192]{1,0:T(8,128)S(1)}, f32[8,8192]{1,0:T(8,128)S(1)}) custom-call(f32[7,8,8192]{2,1,0:T(8,128)S(1)} %bitcast.5, s32[8,8192]{1,0:T(8,128)S(1)} %copy-done.1, f32[8,128]{1,0:T(8,128)S(1)} %get-tuple-element.13.day_in.refs_4_), custom_call_target="tpu_custom_call" | custom-call | tf_op jit(solution)/shard_map/nearest/pallas_call | solution.py:292
  13.6 0.0 collective-permute-done.2.refs_6_.refs_7_
  13.6 0.0 collective-permute-done.4.refs_5_
  13.6 1.2 %shard_map.39.refs_8_ = f32[7,8,8192]{2,1,0:T(8,128)} custom-call(f32[7,8,8192]{2,1,0:T(8,128)S(1)} %get-tuple-element.14.refs_0_, f32[7,8,8192]{2,1,0:T(8,128)S(1)} %get-tuple-element.15.refs_1_, f32[8,8192]{1,0:T(8,128)S(1)} %get-tuple-element.16.refs_2_, f32[8,8192]{1,0:T(8,128)S(1)} %get-tuple-element.17.refs_3_, ...), custom_call_target="tpu_custom_call" | custom-call | tf_op jit(solution)/shard_map/pallas_call | solution.py:306
  14.9 0.9 %collective-permute-done.1.refs_6_ = f32[8,4096]{1,0:T(8,128)S(1)} collective-permute-done((f32[8,4096]{1,0:T(8,128)S(1)}, f32[8,4096]{1,0:T(8,128)S(1)}, u32[]{:S(2)}, u32[]{:S(2)}) %collective-permute-start.1) | collective-permute-done | bytes 131104 | tf_op jit(solution)/shard_map/ppermute | solution.py:365
  15.8 1.2 %shard_map.40 = f32[7,8,8192]{2,1,0:T(8,128)} custom-call(f32[7,8,8192]{2,1,0:T(8,128)S(1)} %get-tuple-element.14.refs_0_, f32[7,8,8192]{2,1,0:T(8,128)S(1)} %get-tuple-element.15.refs_1_, f32[8,8192]{1,0:T(8,128)S(1)} %get-tuple-element.16.refs_2_, f32[8,8192]{1,0:T(8,128)S(1)} %get-tuple-element.17.refs_3_, ...), custom_call_target="tpu_custom_call", output_to_operand_aliasing={{}: (8, {})} | custom-call | tf_op jit(solution)/shard_map/pallas_call | solution.py:306
Async XLA Ops:
  0.0 4.6 %copy-start.1 = (s32[8,8192]{1,0:T(8,128)S(1)}, s32[8,8192]{1,0:T(8,128)}, u32[]{:S(2)}) copy-start(s32[8,8192]{1,0:T(8,128)} %valid.5) | copy-start | bytes 786436
  0.0 4.6 %copy-start = (f32[8,7,8192]{2,0,1:T(8,128)S(1)}, f32[8,7,8192]{2,0,1:T(8,128)}, u32[]{:S(2)}) copy-start(f32[8,7,8192]{2,0,1:T(8,128)} %param.3) | copy-start | bytes 5505028
  1.6 6.5 %collective-permute-start.3 = (f32[8,4096]{1,0:T(8,128)S(1)}, f32[8,4096]{1,0:T(8,128)S(1)}, u32[]{:S(2)}, u32[]{:S(2)}) collective-permute-start(f32[8,4096]{1,0:T(8,128)S(1)} %get-tuple-element.20.own), channel_id=1, source_target_pairs={{0,8},{8,0},{16,24},{24,16},{1,9},{9,1},{17,25},{25,17},{2,10},{10... | collective-permute-start | bytes 393224 | tf_op jit(solution)/shard_map/ppermute | solution.py:365
  4.9 5.7 %collective-permute-start = (f32[8,4096]{1,0:T(8,128)S(1)}, f32[8,4096]{1,0:T(8,128)S(1)}, u32[]{:S(2)}, u32[]{:S(2)}) collective-permute-start(f32[8,4096]{1,0:T(8,128)S(1)} %shard_map.37), channel_id=1, source_target_pairs={{0,16},{8,24},{16,0},{24,8},{1,17},{9,25},{17,1},{25,9},{2,18},{10... | collective-permute-start | bytes 393224 | tf_op jit(solution)/shard_map/ppermute | solution.py:368
  6.9 6.7 %collective-permute-start.2 = (f32[8,4096]{1,0:T(8,128)S(1)}, f32[8,4096]{1,0:T(8,128)S(1)}, u32[]{:S(2)}, u32[]{:S(2)}) collective-permute-start(f32[8,4096]{1,0:T(8,128)S(1)} %get-tuple-element.19), channel_id=1, source_target_pairs={{0,8},{8,0},{16,24},{24,16},{1,9},{9,1},{17,25},{25,17},{2,10},{10... | collective-permute-start | bytes 393224 | tf_op jit(solution)/shard_map/ppermute | solution.py:365
  8.2 5.4 %collective-permute-start.4 = (f32[8,4096]{1,0:T(8,128)S(1)}, f32[8,4096]{1,0:T(8,128)S(1)}, u32[]{:S(2)}, u32[]{:S(2)}) collective-permute-start(f32[8,4096]{1,0:T(8,128)S(1)} %join_first.1), channel_id=1, source_target_pairs={{0,16},{8,24},{16,0},{24,8},{1,17},{9,25},{17,1},{25,9},{2,18},{10... | collective-permute-start | bytes 393224 | tf_op jit(solution)/shard_map/ppermute | solution.py:368
  10.7 5.1 %collective-permute-start.1 = (f32[8,4096]{1,0:T(8,128)S(1)}, f32[8,4096]{1,0:T(8,128)S(1)}, u32[]{:S(2)}, u32[]{:S(2)}) collective-permute-start(f32[8,4096]{1,0:T(8,128)S(1)} %join_second.1), channel_id=1, source_target_pairs={{0,8},{8,0},{16,24},{24,16},{1,9},{9,1},{17,25},{25,17},{2,10},{10... | collective-permute-start | bytes 393224 | tf_op jit(solution)/shard_map/ppermute | solution.py:365

commit v5 on v4

--- a/solution.py
+++ b/solution.py
@@ -9,6 +9,7 @@
 
 
 LANES = 128
+UNROLL = 16
 TOP = 1048576.0
 VMEM = pl.BlockSpec(memory_space=pltpu.VMEM)
 HBM = pl.BlockSpec(memory_space=pltpu.HBM)
@@ -115,10 +116,10 @@
         for c in copies[k]:
             c.wait()
 
-        @pl.loop(0, piece // LANES // 4)
+        @pl.loop(0, piece // LANES // UNROLL)
         def _(j):
-            for u in range(4):
-                cols = span_of(k * (piece // LANES) + j * 4 + u)
+            for u in range(UNROLL):
+                cols = span_of(k * (piece // LANES) + j * UNROLL + u)
                 live = valid[:, cols] > 0
                 values = [refl[b, :, cols] for b in range(bands)]
                 packets = packet_of(values, live, day_col, rows, packet_rows, firsts)
@@ -133,11 +134,11 @@
     _, upper, _ = flags()
     day_col = day_in[...]
 
-    @pl.loop(0, half // LANES // 4)
+    @pl.loop(0, half // LANES // UNROLL)
     def _(j):
-        for u in range(4):
-            cols = span_of(j * 4 + u)
-            far = span_of(half // LANES + j * 4 + u)
+        for u in range(UNROLL):
+            cols = span_of(j * UNROLL + u)
+            far = span_of(half // LANES + j * UNROLL + u)
             live = valid[:, far] > 0
             values = [refl[k, :, far] for k in range(bands)]
             (a,) = packet_of(values, live, day_col, rows, packet_rows, (upper,))
@@ -151,11 +152,11 @@
     odd, _, inner = flags()
     day_col = day_in[...]
 
-    @pl.loop(0, half // LANES // 4)
+    @pl.loop(0, half // LANES // UNROLL)
     def _(j):
-        for u in range(4):
-            cols = span_of(j * 4 + u)
-            far = span_of(half // LANES + j * 4 + u)
+        for u in range(UNROLL):
+            cols = span_of(j * UNROLL + u)
+            far = span_of(half // LANES + j * UNROLL + u)
             live = valid[:, far] > 0
             values = [refl[k, :, far] for k in range(bands)]
             (b,) = packet_of(values, live, day_col, rows, packet_rows, (odd,))
@@ -171,10 +172,10 @@
 
 
 def join_near_kernel(own, got, out):
-    @pl.loop(0, own.shape[1] // LANES // 4)
+    @pl.loop(0, own.shape[1] // LANES // UNROLL)
     def _(j):
-        for u in range(4):
-            cols = span_of(j * 4 + u)
+        for u in range(UNROLL):
+            cols = span_of(j * UNROLL + u)
             a, b = own[:, cols], got[:, cols]
             out[:, cols] = jnp.where(nearness(a) >= nearness(b), a, b)
 
@@ -182,10 +183,10 @@
 def join_own_kernel(own, got, out):
     _, _, inner = flags()
 
-    @pl.loop(0, own.shape[1] // LANES // 4)
+    @pl.loop(0, own.shape[1] // LANES // UNROLL)
     def _(j):
-        for u in range(4):
-            cols = span_of(j * 4 + u)
+        for u in range(UNROLL):
+            cols = span_of(j * UNROLL + u)
             a, b = own[:, cols], got[:, cols]
             use = jnp.logical_and(inner, nearness(a) > 0.0)
             out[:, cols] = jnp.where(use, a, b)
@@ -226,10 +227,10 @@
     rows, _ = tile_rows(bands, count)
     day_col = day_in[...]
 
-    @pl.loop(0, pixels // LANES // 4)
+    @pl.loop(0, pixels // LANES // UNROLL)
     def _(j):
-        for u in range(4):
-            cols = span_of(j * 4 + u)
+        for u in range(UNROLL):
+            cols = span_of(j * UNROLL + u)
             live = valid[:, cols] > 0
             prev_pos = running(jnp.where(live, rows, -1), rows, count, True)
             next_pos = running(jnp.where(live, rows, count), rows, count, False)
@@ -254,10 +255,10 @@
     copies = []
     for k in range(width // piece):
 
-        @pl.loop(0, piece // LANES // 4)
+        @pl.loop(0, piece // LANES // 8)
         def _(j):
-            for u in range(4):
-                i = k * (piece // LANES) + j * 4 + u
+            for u in range(8):
+                i = k * (piece // LANES) + j * 8 + u
                 cols = span_of(i)
                 far = span_of(start // LANES + i)
                 before, after = merge(gots, cols)
@@ -339,7 +340,7 @@
 
 def body_any(devices, reflectance, validity, day_number):
     pixels = reflectance.shape[2]
-    piece = pixels // 8
+    piece = pixels // 4
     stack = jnp.transpose(reflectance, (1, 0, 2))
     bits = list(range((devices - 1).bit_length()))
     day_col, *sends = load(piece, pixels, bits, day_number, stack, validity)
@@ -367,7 +368,7 @@
     def along(x):
         return lax.ppermute(x, "date", [(d, d ^ 2) for d in range(4)])
 
-    day_col, sy1 = load(piece, half, (1,), day_number, stack, validity)
+    day_col, sy1 = load(half // 2, half, (1,), day_number, stack, validity)
     refl, valid = stack, validity
     got1 = across(sy1)
 

time: 17.2 us -> 17 us (0.988)
  Pallas kernels: 5.67 us -> 4.91 us
  waiting for transfers between devices: 1.54 us -> 2.12 us
    pallas_call x2, Pallas kernels: 2.49 us -> 2.14 us  [fill(): pl.pallas_call(functools.partial(fill_kernel, start, width, piece, len(go...]
    ppermute x3, waiting for transfers between devices: 1.54 us -> 1.86 us  [across(): return lax.ppermute(x, 'date', [(d, d ^ 1) for d in range(4)])]
    ppermute x2, waiting for transfers between devices: 0.01 us -> 0.26 us  [along(): return lax.ppermute(x, 'date', [(d, d ^ 2) for d in range(4)])]
  transfers between devices with their start and end apart: 5 -> 5, of which waited for: 2 -> 3; matrix products, arithmetic and copies ran while one was open for 0% -> 0% of each run, Pallas kernels for 17% -> 14%
where the time goes in v5:
time: 17 us; the launch traced here: 16.8 us
  starting transfers between devices  9.74 us (57%)
  Pallas kernels  4.91 us (29%)
  waiting for transfers between devices  2.12 us (12%)
    ppermute x3, starting transfers between devices, across(): return lax.ppermute(x, 'date', [(d, d ^ 1) for d in range(4)])  5.61 us
    ppermute x2, starting transfers between devices, along(): return lax.ppermute(x, 'date', [(d, d ^ 2) for d in range(4)])  4.13 us
    pallas_call x2, Pallas kernels, fill(): pl.pallas_call(functools.partial(fill_kernel, start, width, piece, len(go...  2.14 us
    ppermute x3, waiting for transfers between devices, across(): return lax.ppermute(x, 'date', [(d, d ^ 1) for d in range(4)])  1.86 us
    pallas_call x1, Pallas kernels, load(): pl.pallas_call(functools.partial(load_kernel, piece, bits), in_specs=[HBM...  1.5 us
    pallas_call x1, Pallas kernels, nearest(): pl.pallas_call(near_kernel, in_specs=[VMEM] * 3, out_specs=[VMEM] * 4, ou...  0.62 us
    pallas_call x2, Pallas kernels, packets(): pl.pallas_call(kernel, in_specs=[VMEM] * 3, out_specs=[VMEM] * results, o...  0.51 us
  transfers between devices with their start and end apart: 5, of which 3 were waited for; matrix products, arithmetic and copies ran while one was open for 0% of the time, Pallas kernels for 14%

profile of v5, /device:TPU:0, one launch (start us, length us, event | category | flops | bytes accessed | tf_op | source)
XLA Modules:
  0.0 16.8 jit_solution(13791530963774774790)
XLA Ops:
  0.0 0.0 copy-start.1
  0.0 0.0 copy-start
  0.0 1.5 %load.1 = (f32[8,128]{1,0:T(8,128)S(1)}, f32[8,4096]{1,0:T(8,128)S(1)}) custom-call(s32[8]{0:T(128)} %days_in.1, f32[7,8,8192]{2,1,0:T(8,128)} %bitcast.2, s32[8,8192]{1,0:T(8,128)} %valid.5), custom_call_target="tpu_custom_call" | custom-call | tf_op jit(solution)/shard_map/load/pallas_call | solution.py:324
  1.5 3.0 %collective-permute-start.3 = (f32[8,4096]{1,0:T(8,128)S(1)}, f32[8,4096]{1,0:T(8,128)S(1)}, u32[]{:S(2)}, u32[]{:S(2)}) collective-permute-start(f32[8,4096]{1,0:T(8,128)S(1)} %get-tuple-element.20.own), channel_id=1, source_target_pairs={{0,8},{8,0},{16,24},{24,16},{1,9},{9,1},{17,25},{25,17},{2,10},{10... | collective-permute-start | bytes 393224 | tf_op jit(solution)/shard_map/ppermute | solution.py:366
  4.5 0.0 copy-done.1
  4.5 0.0 copy-done
  4.6 0.2 %shard_map.37 = f32[8,4096]{1,0:T(8,128)S(1)} custom-call(f32[7,8,8192]{2,1,0:T(8,128)S(1)} %bitcast.3, s32[8,8192]{1,0:T(8,128)S(1)} %copy-done.1, f32[8,128]{1,0:T(8,128)S(1)} %get-tuple-element.13.day_in.refs_4_), custom_call_target="tpu_custom_call" | custom-call | tf_op jit(solution)/shard_map/pallas_call | solution.py:376
  4.7 1.6 %collective-permute-start = (f32[8,4096]{1,0:T(8,128)S(1)}, f32[8,4096]{1,0:T(8,128)S(1)}, u32[]{:S(2)}, u32[]{:S(2)}) collective-permute-start(f32[8,4096]{1,0:T(8,128)S(1)} %shard_map.37), channel_id=1, source_target_pairs={{0,16},{8,24},{16,0},{24,8},{1,17},{9,25},{17,1},{25,9},{2,18},{10... | collective-permute-start | bytes 393224 | tf_op jit(solution)/shard_map/ppermute | solution.py:369
  6.3 0.3 %shard_map.38 = (f32[8,4096]{1,0:T(8,128)S(1)}, f32[8,4096]{1,0:T(8,128)S(1)}) custom-call(f32[7,8,8192]{2,1,0:T(8,128)S(1)} %bitcast.4, s32[8,8192]{1,0:T(8,128)S(1)} %copy-done.1, f32[8,128]{1,0:T(8,128)S(1)} %get-tuple-element.13.day_in.refs_4_), custom_call_target="tpu_custom_call" | custom-call | tf_op jit(solution)/shard_map/pallas_call | solution.py:376
  6.7 0.6 %collective-permute-start.2 = (f32[8,4096]{1,0:T(8,128)S(1)}, f32[8,4096]{1,0:T(8,128)S(1)}, u32[]{:S(2)}, u32[]{:S(2)}) collective-permute-start(f32[8,4096]{1,0:T(8,128)S(1)} %get-tuple-element.19), channel_id=1, source_target_pairs={{0,8},{8,0},{16,24},{24,16},{1,9},{9,1},{17,25},{25,17},{2,10},{10... | collective-permute-start | bytes 393224 | tf_op jit(solution)/shard_map/ppermute | solution.py:366
  7.3 0.8 %collective-permute-done.3.got.refs_7_ = f32[8,4096]{1,0:T(8,128)S(1)} collective-permute-done((f32[8,4096]{1,0:T(8,128)S(1)}, f32[8,4096]{1,0:T(8,128)S(1)}, u32[]{:S(2)}, u32[]{:S(2)}) %collective-permute-start.3) | collective-permute-done | bytes 131104 | tf_op jit(solution)/shard_map/ppermute | solution.py:366
  8.0 0.1 join_first.1
  8.1 2.5 %collective-permute-start.4 = (f32[8,4096]{1,0:T(8,128)S(1)}, f32[8,4096]{1,0:T(8,128)S(1)}, u32[]{:S(2)}, u32[]{:S(2)}) collective-permute-start(f32[8,4096]{1,0:T(8,128)S(1)} %join_first.1), channel_id=1, source_target_pairs={{0,16},{8,24},{16,0},{24,8},{1,17},{9,25},{17,1},{25,9},{2,18},{10... | collective-permute-start | bytes 393224 | tf_op jit(solution)/shard_map/ppermute | solution.py:369
  10.7 0.0 collective-permute-done.got.refs_5_
  10.7 0.1 join_second.1
  10.7 2.0 %collective-permute-start.1 = (f32[8,4096]{1,0:T(8,128)S(1)}, f32[8,4096]{1,0:T(8,128)S(1)}, u32[]{:S(2)}, u32[]{:S(2)}) collective-permute-start(f32[8,4096]{1,0:T(8,128)S(1)} %join_second.1), channel_id=1, source_target_pairs={{0,8},{8,0},{16,24},{24,16},{1,9},{9,1},{17,25},{25,17},{2,10},{10... | collective-permute-start | bytes 393224 | tf_op jit(solution)/shard_map/ppermute | solution.py:366
  12.7 0.6 %nearest.1 = (f32[7,8,8192]{2,1,0:T(8,128)S(1)}, f32[7,8,8192]{2,1,0:T(8,128)S(1)}, f32[8,8192]{1,0:T(8,128)S(1)}, f32[8,8192]{1,0:T(8,128)S(1)}) custom-call(f32[7,8,8192]{2,1,0:T(8,128)S(1)} %bitcast.5, s32[8,8192]{1,0:T(8,128)S(1)} %copy-done.1, f32[8,128]{1,0:T(8,128)S(1)} %get-tuple-element.13.day_in.refs_4_), custom_call_target="tpu_custom_call" | custom-call | tf_op jit(solution)/shard_map/nearest/pallas_call | solution.py:293
  13.3 0.0 collective-permute-done.2.refs_6_.refs_7_
  13.3 0.3 %collective-permute-done.4.refs_5_ = f32[8,4096]{1,0:T(8,128)S(1)} collective-permute-done((f32[8,4096]{1,0:T(8,128)S(1)}, f32[8,4096]{1,0:T(8,128)S(1)}, u32[]{:S(2)}, u32[]{:S(2)}) %collective-permute-start.4) | collective-permute-done | bytes 131104 | tf_op jit(solution)/shard_map/ppermute | solution.py:369
  13.6 1.1 %shard_map.39.refs_8_ = f32[7,8,8192]{2,1,0:T(8,128)} custom-call(f32[7,8,8192]{2,1,0:T(8,128)S(1)} %get-tuple-element.14.refs_0_, f32[7,8,8192]{2,1,0:T(8,128)S(1)} %get-tuple-element.15.refs_1_, f32[8,8192]{1,0:T(8,128)S(1)} %get-tuple-element.16.refs_2_, f32[8,8192]{1,0:T(8,128)S(1)} %get-tuple-element.17.refs_3_, ...), custom_call_target="tpu_custom_call" | custom-call | tf_op jit(solution)/shard_map/pallas_call | solution.py:307
  14.7 1.1 %collective-permute-done.1.refs_6_ = f32[8,4096]{1,0:T(8,128)S(1)} collective-permute-done((f32[8,4096]{1,0:T(8,128)S(1)}, f32[8,4096]{1,0:T(8,128)S(1)}, u32[]{:S(2)}, u32[]{:S(2)}) %collective-permute-start.1) | collective-permute-done | bytes 131104 | tf_op jit(solution)/shard_map/ppermute | solution.py:366
  15.8 1.1 %shard_map.40 = f32[7,8,8192]{2,1,0:T(8,128)} custom-call(f32[7,8,8192]{2,1,0:T(8,128)S(1)} %get-tuple-element.14.refs_0_, f32[7,8,8192]{2,1,0:T(8,128)S(1)} %get-tuple-element.15.refs_1_, f32[8,8192]{1,0:T(8,128)S(1)} %get-tuple-element.16.refs_2_, f32[8,8192]{1,0:T(8,128)S(1)} %get-tuple-element.17.refs_3_, ...), custom_call_target="tpu_custom_call", output_to_operand_aliasing={{}: (8, {})} | custom-call | tf_op jit(solution)/shard_map/pallas_call | solution.py:307
Async XLA Ops:
  0.0 4.5 %copy-start.1 = (s32[8,8192]{1,0:T(8,128)S(1)}, s32[8,8192]{1,0:T(8,128)}, u32[]{:S(2)}) copy-start(s32[8,8192]{1,0:T(8,128)} %valid.5) | copy-start | bytes 786436
  0.0 4.5 %copy-start = (f32[8,7,8192]{2,0,1:T(8,128)S(1)}, f32[8,7,8192]{2,0,1:T(8,128)}, u32[]{:S(2)}) copy-start(f32[8,7,8192]{2,0,1:T(8,128)} %param.3) | copy-start | bytes 5505028
  1.5 6.5 %collective-permute-start.3 = (f32[8,4096]{1,0:T(8,128)S(1)}, f32[8,4096]{1,0:T(8,128)S(1)}, u32[]{:S(2)}, u32[]{:S(2)}) collective-permute-start(f32[8,4096]{1,0:T(8,128)S(1)} %get-tuple-element.20.own), channel_id=1, source_target_pairs={{0,8},{8,0},{16,24},{24,16},{1,9},{9,1},{17,25},{25,17},{2,10},{10... | collective-permute-start | bytes 393224 | tf_op jit(solution)/shard_map/ppermute | solution.py:366
  4.7 5.9 %collective-permute-start = (f32[8,4096]{1,0:T(8,128)S(1)}, f32[8,4096]{1,0:T(8,128)S(1)}, u32[]{:S(2)}, u32[]{:S(2)}) collective-permute-start(f32[8,4096]{1,0:T(8,128)S(1)} %shard_map.37), channel_id=1, source_target_pairs={{0,16},{8,24},{16,0},{24,8},{1,17},{9,25},{17,1},{25,9},{2,18},{10... | collective-permute-start | bytes 393224 | tf_op jit(solution)/shard_map/ppermute | solution.py:369
  6.7 6.7 %collective-permute-start.2 = (f32[8,4096]{1,0:T(8,128)S(1)}, f32[8,4096]{1,0:T(8,128)S(1)}, u32[]{:S(2)}, u32[]{:S(2)}) collective-permute-start(f32[8,4096]{1,0:T(8,128)S(1)} %get-tuple-element.19), channel_id=1, source_target_pairs={{0,8},{8,0},{16,24},{24,16},{1,9},{9,1},{17,25},{25,17},{2,10},{10... | collective-permute-start | bytes 393224 | tf_op jit(solution)/shard_map/ppermute | solution.py:366
  8.1 5.5 %collective-permute-start.4 = (f32[8,4096]{1,0:T(8,128)S(1)}, f32[8,4096]{1,0:T(8,128)S(1)}, u32[]{:S(2)}, u32[]{:S(2)}) collective-permute-start(f32[8,4096]{1,0:T(8,128)S(1)} %join_first.1), channel_id=1, source_target_pairs={{0,16},{8,24},{16,0},{24,8},{1,17},{9,25},{17,1},{25,9},{2,18},{10... | collective-permute-start | bytes 393224 | tf_op jit(solution)/shard_map/ppermute | solution.py:369
  10.7 5.0 %collective-permute-start.1 = (f32[8,4096]{1,0:T(8,128)S(1)}, f32[8,4096]{1,0:T(8,128)S(1)}, u32[]{:S(2)}, u32[]{:S(2)}) collective-permute-start(f32[8,4096]{1,0:T(8,128)S(1)} %join_second.1), channel_id=1, source_target_pairs={{0,8},{8,0},{16,24},{24,16},{1,9},{9,1},{17,25},{25,17},{2,10},{10... | collective-permute-start | bytes 393224 | tf_op jit(solution)/shard_map/ppermute | solution.py:366

commit v6 on v5

--- a/solution.py
+++ b/solution.py
@@ -47,6 +47,20 @@
 
 def span_of(i):
     return pl.ds(pl.multiple_of(i * LANES, LANES), LANES)
+
+
+def each_tile(tiles, most=UNROLL):
+    def run(work):
+        if tiles == 0:
+            return
+        step = max(u for u in range(1, most + 1) if tiles % u == 0)
+
+        @pl.loop(0, tiles // step)
+        def _(j):
+            for u in range(step):
+                work(j * step + u)
+
+    return run
 
 
 def packet_of(values, live, day_col, rows, packet_rows, firsts):
@@ -116,55 +130,62 @@
         for c in copies[k]:
             c.wait()
 
-        @pl.loop(0, piece // LANES // UNROLL)
-        def _(j):
-            for u in range(UNROLL):
-                cols = span_of(k * (piece // LANES) + j * UNROLL + u)
-                live = valid[:, cols] > 0
-                values = [refl[b, :, cols] for b in range(bands)]
-                packets = packet_of(values, live, day_col, rows, packet_rows, firsts)
-                for send, packet in zip(sends, packets):
-                    send[:, cols] = packet
+        @each_tile(piece // LANES)
+        def _(i):
+            cols = span_of(k * (piece // LANES) + i)
+            live = valid[:, cols] > 0
+            values = [refl[b, :, cols] for b in range(bands)]
+            packets = packet_of(values, live, day_col, rows, packet_rows, firsts)
+            for send, packet in zip(sends, packets):
+                send[:, cols] = packet
 
 
 def second_kernel(refl, valid, day_in, sy):
     bands, count, pixels = refl.shape
-    half = pixels // 2
+    tiles = sy.shape[1] // LANES
     rows, packet_rows = tile_rows(bands, count)
     _, upper, _ = flags()
     day_col = day_in[...]
 
-    @pl.loop(0, half // LANES // UNROLL)
-    def _(j):
-        for u in range(UNROLL):
-            cols = span_of(j * UNROLL + u)
-            far = span_of(half // LANES + j * UNROLL + u)
-            live = valid[:, far] > 0
-            values = [refl[k, :, far] for k in range(bands)]
-            (a,) = packet_of(values, live, day_col, rows, packet_rows, (upper,))
-            sy[:, cols] = a
+    @each_tile(tiles)
+    def _(i):
+        cols = span_of(i)
+        far = span_of(pixels // LANES - tiles + i)
+        live = valid[:, far] > 0
+        values = [refl[k, :, far] for k in range(bands)]
+        (a,) = packet_of(values, live, day_col, rows, packet_rows, (upper,))
+        sy[:, cols] = a
 
 
 def side_kernel(refl, valid, day_in, sx, side):
     bands, count, pixels = refl.shape
-    half = pixels // 2
+    seconds = sx.shape[1] // LANES
+    firsts = pixels // LANES - seconds
     rows, packet_rows = tile_rows(bands, count)
     odd, _, inner = flags()
     day_col = day_in[...]
 
-    @pl.loop(0, half // LANES // UNROLL)
-    def _(j):
-        for u in range(UNROLL):
-            cols = span_of(j * UNROLL + u)
-            far = span_of(half // LANES + j * UNROLL + u)
-            live = valid[:, far] > 0
-            values = [refl[k, :, far] for k in range(bands)]
-            (b,) = packet_of(values, live, day_col, rows, packet_rows, (odd,))
-            sx[:, cols] = b
-            live = valid[:, cols] > 0
-            values = [refl[k, :, cols] for k in range(bands)]
-            (c,) = packet_of(values, live, day_col, rows, packet_rows, (odd,))
-            side[:, cols] = jnp.where(inner, c, b)
+    def made(cols):
+        live = valid[:, cols] > 0
+        values = [refl[k, :, cols] for k in range(bands)]
+        return packet_of(values, live, day_col, rows, packet_rows, (odd,))[0]
+
+    @each_tile(min(firsts, seconds))
+    def _(i):
+        cols = span_of(i)
+        far = made(span_of(firsts + i))
+        sx[:, cols] = far
+        side[:, cols] = jnp.where(inner, made(cols), far)
+
+    @each_tile(abs(firsts - seconds))
+    def _(i):
+        cols = span_of(min(firsts, seconds) + i)
+        if firsts > seconds:
+            side[:, cols] = made(cols)
+        else:
+            far = made(span_of(firsts + firsts + i))
+            sx[:, cols] = far
+            side[:, cols] = far
 
 
 def nearness(packet):
@@ -172,24 +193,22 @@
 
 
 def join_near_kernel(own, got, out):
-    @pl.loop(0, own.shape[1] // LANES // UNROLL)
-    def _(j):
-        for u in range(UNROLL):
-            cols = span_of(j * UNROLL + u)
-            a, b = own[:, cols], got[:, cols]
-            out[:, cols] = jnp.where(nearness(a) >= nearness(b), a, b)
+    @each_tile(own.shape[1] // LANES)
+    def _(i):
+        cols = span_of(i)
+        a, b = own[:, cols], got[:, cols]
+        out[:, cols] = jnp.where(nearness(a) >= nearness(b), a, b)
 
 
 def join_own_kernel(own, got, out):
     _, _, inner = flags()
 
-    @pl.loop(0, own.shape[1] // LANES // UNROLL)
-    def _(j):
-        for u in range(UNROLL):
-            cols = span_of(j * UNROLL + u)
-            a, b = own[:, cols], got[:, cols]
-            use = jnp.logical_and(inner, nearness(a) > 0.0)
-            out[:, cols] = jnp.where(use, a, b)
+    @each_tile(own.shape[1] // LANES)
+    def _(i):
+        cols = span_of(i)
+        a, b = own[:, cols], got[:, cols]
+        use = jnp.logical_and(inner, nearness(a) > 0.0)
+        out[:, cols] = jnp.where(use, a, b)
 
 
 def merge_first(refs, cols):
@@ -227,23 +246,22 @@
     rows, _ = tile_rows(bands, count)
     day_col = day_in[...]
 
-    @pl.loop(0, pixels // LANES // UNROLL)
-    def _(j):
-        for u in range(UNROLL):
-            cols = span_of(j * UNROLL + u)
-            live = valid[:, cols] > 0
-            prev_pos = running(jnp.where(live, rows, -1), rows, count, True)
-            next_pos = running(jnp.where(live, rows, count), rows, count, False)
-            prev_in = prev_pos >= 0
-            next_in = next_pos < count
-            prev_pos = prev_pos & (count - 1)
-            next_pos = next_pos & (count - 1)
-            prev_days[:, cols] = jnp.where(prev_in, pick(day_col, prev_pos), 0.0)
-            next_days[:, cols] = jnp.where(next_in, pick(day_col, next_pos), TOP)
-            for b in range(bands):
-                x = refl[b, :, cols]
-                prev_out[b, :, cols] = pick(x, prev_pos)
-                next_out[b, :, cols] = pick(x, next_pos)
+    @each_tile(pixels // LANES)
+    def _(i):
+        cols = span_of(i)
+        live = valid[:, cols] > 0
+        prev_pos = running(jnp.where(live, rows, -1), rows, count, True)
+        next_pos = running(jnp.where(live, rows, count), rows, count, False)
+        prev_in = prev_pos >= 0
+        next_in = next_pos < count
+        prev_pos = prev_pos & (count - 1)
+        next_pos = next_pos & (count - 1)
+        prev_days[:, cols] = jnp.where(prev_in, pick(day_col, prev_pos), 0.0)
+        next_days[:, cols] = jnp.where(next_in, pick(day_col, next_pos), TOP)
+        for b in range(bands):
+            x = refl[b, :, cols]
+            prev_out[b, :, cols] = pick(x, prev_pos)
+            next_out[b, :, cols] = pick(x, next_pos)
 
 
 def fill_kernel(start, width, piece, packets, merge, *refs):
@@ -255,27 +273,26 @@
     copies = []
     for k in range(width // piece):
 
-        @pl.loop(0, piece // LANES // 8)
-        def _(j):
-            for u in range(8):
-                i = k * (piece // LANES) + j * 8 + u
-                cols = span_of(i)
-                far = span_of(start // LANES + i)
-                before, after = merge(gots, cols)
-                prev_day, next_day = prev_days[:, far], next_days[:, far]
-                prev_in, next_in = prev_day > 0.0, next_day < TOP
-                prev_day = jnp.where(prev_in, prev_day, before[bands:])
-                next_day = jnp.where(next_in, next_day, TOP - after[bands:])
-                has_prev = prev_day > 0.0
-                both = jnp.logical_and(has_prev, next_day < TOP)
-                span = jnp.maximum(jnp.where(both, next_day - prev_day, 1.0), 1.0)
-                weight = jnp.where(
-                    both, (day_col - prev_day) / span, jnp.where(has_prev, 0.0, 1.0)
-                )
-                for b in range(bands):
-                    prev = jnp.where(prev_in, prev_own[b, :, far], before[b : b + 1])
-                    nxt = jnp.where(next_in, next_own[b, :, far], after[b : b + 1])
-                    buf[b, :, cols] = prev + weight * (nxt - prev)
+        @each_tile(piece // LANES, 10)
+        def _(i):
+            i = k * (piece // LANES) + i
+            cols = span_of(i)
+            far = span_of(start // LANES + i)
+            before, after = merge(gots, cols)
+            prev_day, next_day = prev_days[:, far], next_days[:, far]
+            prev_in, next_in = prev_day > 0.0, next_day < TOP
+            prev_day = jnp.where(prev_in, prev_day, before[bands:])
+            next_day = jnp.where(next_in, next_day, TOP - after[bands:])
+            has_prev = prev_day > 0.0
+            both = jnp.logical_and(has_prev, next_day < TOP)
+            span = jnp.maximum(jnp.where(both, next_day - prev_day, 1.0), 1.0)
+            weight = jnp.where(
+                both, (day_col - prev_day) / span, jnp.where(has_prev, 0.0, 1.0)
+            )
+            for b in range(bands):
+                prev = jnp.where(prev_in, prev_own[b, :, far], before[b : b + 1])
+                nxt = jnp.where(next_in, next_own[b, :, far], after[b : b + 1])
+                buf[b, :, cols] = prev + weight * (nxt - prev)
 
         copy = pltpu.make_async_copy(
             buf.at[:, :, pl.ds(k * piece, piece)],
@@ -338,6 +355,10 @@
     )(*args)
 
 
+def pieces_of(width, most):
+    return width // max(n for n in range(1, most + 1) if width % (n * LANES) == 0)
+
+
 def body_any(devices, reflectance, validity, day_number):
     pixels = reflectance.shape[2]
     piece = pixels // 4
@@ -357,10 +378,9 @@
 
 def body(reflectance, validity, day_number):
     _, bands, pixels = reflectance.shape
-    half = pixels // 2
-    piece = half // 4
+    first = pixels // LANES * 8 // 16 * LANES
+    second = pixels - first
     stack = jnp.transpose(reflectance, (1, 0, 2))
-    packet = f32(bands + 1, half)
 
     def across(x):
         return lax.ppermute(x, "date", [(d, d ^ 1) for d in range(4)])
@@ -368,33 +388,40 @@
     def along(x):
         return lax.ppermute(x, "date", [(d, d ^ 2) for d in range(4)])
 
-    day_col, sy1 = load(half // 2, half, (1,), day_number, stack, validity)
+    day_col, sy1 = load(pieces_of(first, 2), first, (1,), day_number, stack, validity)
     refl, valid = stack, validity
     got1 = across(sy1)
 
-    def packets(kernel, results):
+    def packets(kernel, widths):
         return pl.pallas_call(
             kernel,
             in_specs=[VMEM] * 3,
-            out_specs=[VMEM] * results,
-            out_shape=[packet] * results,
+            out_specs=[VMEM] * len(widths),
+            out_shape=[f32(bands + 1, w) for w in widths],
             compiler_params=PARAMS,
         )(refl, valid, day_col)
 
-    (sy2,) = packets(second_kernel, 1)
+    (sy2,) = packets(second_kernel, [second])
     got2 = along(sy2)
-    sx2, side = packets(side_kernel, 2)
+    sx2, side = packets(side_kernel, [second, max(first, second)])
     side = across(side)
-    join = dict(
-        in_specs=[VMEM] * 2, out_specs=VMEM, out_shape=packet, compiler_params=PARAMS
-    )
-    joined1 = pl.pallas_call(join_near_kernel, name="join_first", **join)(sy1, got1)
-    far1 = along(joined1)
-    joined2 = pl.pallas_call(join_own_kernel, name="join_second", **join)(sx2, got2)
-    far2 = across(joined2)
+
+    def join(kernel, own, got):
+        return pl.pallas_call(
+            kernel,
+            in_specs=[VMEM] * 2,
+            out_specs=VMEM,
+            out_shape=f32(*own.shape),
+            compiler_params=PARAMS,
+        )(own, got)
+
+    far1 = along(join(join_near_kernel, sy1, got1))
+    far2 = across(join(join_own_kernel, sx2, got2))
     arrays = (nearest(refl, valid, day_col), day_col)
+    piece = pieces_of(first, 4)
     out = fill(0, piece, merge_first, *arrays, (far1, side, got1))
-    out = fill(half, piece, merge_second, *arrays, (got2, far2, side), out)
+    piece = pieces_of(second, 4)
+    out = fill(first, piece, merge_second, *arrays, (got2, far2, side), out)
     return jnp.transpose(out, (1, 0, 2))
 
 

time: 17 us -> 17 us (level)
  no operation moved by 1% of the time
where the time goes in v6:
time: 17 us; the launch traced here: 16.8 us
  starting transfers between devices  9.74 us (57%)
  Pallas kernels  4.91 us (29%)
  waiting for transfers between devices  2.12 us (12%)
    ppermute x3, starting transfers between devices, across(): return lax.ppermute(x, 'date', [(d, d ^ 1) for d in range(4)])  5.61 us
    ppermute x2, starting transfers between devices, along(): return lax.ppermute(x, 'date', [(d, d ^ 2) for d in range(4)])  4.13 us
    pallas_call x2, Pallas kernels, fill(): pl.pallas_call(functools.partial(fill_kernel, start, width, piece, len(go...  2.14 us
    ppermute x3, waiting for transfers between devices, across(): return lax.ppermute(x, 'date', [(d, d ^ 1) for d in range(4)])  1.86 us
    pallas_call x1, Pallas kernels, load(): pl.pallas_call(functools.partial(load_kernel, piece, bits), in_specs=[HBM...  1.5 us
    pallas_call x1, Pallas kernels, nearest(): pl.pallas_call(near_kernel, in_specs=[VMEM] * 3, out_specs=[VMEM] * 4, ou...  0.62 us
    pallas_call x2, Pallas kernels, packets(): pl.pallas_call(kernel, in_specs=[VMEM] * 3, out_specs=[VMEM] * len(widths...  0.51 us
  transfers between devices with their start and end apart: 5, of which 3 were waited for; matrix products, arithmetic and copies ran while one was open for 0% of the time, Pallas kernels for 14%

profile of v6, /device:TPU:0, one launch (start us, length us, event | category | flops | bytes accessed | tf_op | source)
XLA Modules:
  0.0 16.8 jit_solution(13791530963774774790)
XLA Ops:
  0.0 0.0 copy-start.1
  0.0 0.0 copy-start
  0.0 1.5 %load.1 = (f32[8,128]{1,0:T(8,128)S(1)}, f32[8,4096]{1,0:T(8,128)S(1)}) custom-call(s32[8]{0:T(128)} %days_in.1, f32[7,8,8192]{2,1,0:T(8,128)} %bitcast.2, s32[8,8192]{1,0:T(8,128)} %valid.5), custom_call_target="tpu_custom_call" | custom-call | tf_op jit(solution)/shard_map/load/pallas_call | solution.py:341
  1.5 3.0 %collective-permute-start.3 = (f32[8,4096]{1,0:T(8,128)S(1)}, f32[8,4096]{1,0:T(8,128)S(1)}, u32[]{:S(2)}, u32[]{:S(2)}) collective-permute-start(f32[8,4096]{1,0:T(8,128)S(1)} %get-tuple-element.20.own), channel_id=1, source_target_pairs={{0,8},{8,0},{16,24},{24,16},{1,9},{9,1},{17,25},{25,17},{2,10},{10... | collective-permute-start | bytes 393224 | tf_op jit(solution)/shard_map/ppermute | solution.py:386
  4.5 0.0 copy-done.1
  4.5 0.0 copy-done
  4.6 0.2 %shard_map.37 = f32[8,4096]{1,0:T(8,128)S(1)} custom-call(f32[7,8,8192]{2,1,0:T(8,128)S(1)} %bitcast.3, s32[8,8192]{1,0:T(8,128)S(1)} %copy-done.1, f32[8,128]{1,0:T(8,128)S(1)} %get-tuple-element.13.day_in.refs_4_), custom_call_target="tpu_custom_call" | custom-call | tf_op jit(solution)/shard_map/pallas_call | solution.py:396
  4.7 1.6 %collective-permute-start = (f32[8,4096]{1,0:T(8,128)S(1)}, f32[8,4096]{1,0:T(8,128)S(1)}, u32[]{:S(2)}, u32[]{:S(2)}) collective-permute-start(f32[8,4096]{1,0:T(8,128)S(1)} %shard_map.37), channel_id=1, source_target_pairs={{0,16},{8,24},{16,0},{24,8},{1,17},{9,25},{17,1},{25,9},{2,18},{10... | collective-permute-start | bytes 393224 | tf_op jit(solution)/shard_map/ppermute | solution.py:389
  6.3 0.3 %shard_map.38 = (f32[8,4096]{1,0:T(8,128)S(1)}, f32[8,4096]{1,0:T(8,128)S(1)}) custom-call(f32[7,8,8192]{2,1,0:T(8,128)S(1)} %bitcast.4, s32[8,8192]{1,0:T(8,128)S(1)} %copy-done.1, f32[8,128]{1,0:T(8,128)S(1)} %get-tuple-element.13.day_in.refs_4_), custom_call_target="tpu_custom_call" | custom-call | tf_op jit(solution)/shard_map/pallas_call | solution.py:396
  6.7 0.6 %collective-permute-start.2 = (f32[8,4096]{1,0:T(8,128)S(1)}, f32[8,4096]{1,0:T(8,128)S(1)}, u32[]{:S(2)}, u32[]{:S(2)}) collective-permute-start(f32[8,4096]{1,0:T(8,128)S(1)} %get-tuple-element.19), channel_id=1, source_target_pairs={{0,8},{8,0},{16,24},{24,16},{1,9},{9,1},{17,25},{25,17},{2,10},{10... | collective-permute-start | bytes 393224 | tf_op jit(solution)/shard_map/ppermute | solution.py:386
  7.3 0.8 %collective-permute-done.3.got.refs_7_ = f32[8,4096]{1,0:T(8,128)S(1)} collective-permute-done((f32[8,4096]{1,0:T(8,128)S(1)}, f32[8,4096]{1,0:T(8,128)S(1)}, u32[]{:S(2)}, u32[]{:S(2)}) %collective-permute-start.3) | collective-permute-done | bytes 131104 | tf_op jit(solution)/shard_map/ppermute | solution.py:386
  8.0 0.1 shard_map.40
  8.1 2.5 %collective-permute-start.4 = (f32[8,4096]{1,0:T(8,128)S(1)}, f32[8,4096]{1,0:T(8,128)S(1)}, u32[]{:S(2)}, u32[]{:S(2)}) collective-permute-start(f32[8,4096]{1,0:T(8,128)S(1)} %shard_map.40), channel_id=1, source_target_pairs={{0,16},{8,24},{16,0},{24,8},{1,17},{9,25},{17,1},{25,9},{2,18},{10... | collective-permute-start | bytes 393224 | tf_op jit(solution)/shard_map/ppermute | solution.py:389
  10.7 0.0 collective-permute-done.got.refs_5_
  10.7 0.1 shard_map.39
  10.7 2.0 %collective-permute-start.1 = (f32[8,4096]{1,0:T(8,128)S(1)}, f32[8,4096]{1,0:T(8,128)S(1)}, u32[]{:S(2)}, u32[]{:S(2)}) collective-permute-start(f32[8,4096]{1,0:T(8,128)S(1)} %shard_map.39), channel_id=1, source_target_pairs={{0,8},{8,0},{16,24},{24,16},{1,9},{9,1},{17,25},{25,17},{2,10},{10... | collective-permute-start | bytes 393224 | tf_op jit(solution)/shard_map/ppermute | solution.py:386
  12.7 0.6 %nearest.1 = (f32[7,8,8192]{2,1,0:T(8,128)S(1)}, f32[7,8,8192]{2,1,0:T(8,128)S(1)}, f32[8,8192]{1,0:T(8,128)S(1)}, f32[8,8192]{1,0:T(8,128)S(1)}) custom-call(f32[7,8,8192]{2,1,0:T(8,128)S(1)} %bitcast.5, s32[8,8192]{1,0:T(8,128)S(1)} %copy-done.1, f32[8,128]{1,0:T(8,128)S(1)} %get-tuple-element.13.day_in.refs_4_), custom_call_target="tpu_custom_call" | custom-call | tf_op jit(solution)/shard_map/nearest/pallas_call | solution.py:310
  13.3 0.0 collective-permute-done.2.refs_6_.refs_7_
  13.3 0.3 %collective-permute-done.4.refs_5_ = f32[8,4096]{1,0:T(8,128)S(1)} collective-permute-done((f32[8,4096]{1,0:T(8,128)S(1)}, f32[8,4096]{1,0:T(8,128)S(1)}, u32[]{:S(2)}, u32[]{:S(2)}) %collective-permute-start.4) | collective-permute-done | bytes 131104 | tf_op jit(solution)/shard_map/ppermute | solution.py:389
  13.6 1.1 %shard_map.41.refs_8_ = f32[7,8,8192]{2,1,0:T(8,128)} custom-call(f32[7,8,8192]{2,1,0:T(8,128)S(1)} %get-tuple-element.14.refs_0_, f32[7,8,8192]{2,1,0:T(8,128)S(1)} %get-tuple-element.15.refs_1_, f32[8,8192]{1,0:T(8,128)S(1)} %get-tuple-element.16.refs_2_, f32[8,8192]{1,0:T(8,128)S(1)} %get-tuple-element.17.refs_3_, ...), custom_call_target="tpu_custom_call" | custom-call | tf_op jit(solution)/shard_map/pallas_call | solution.py:324
  14.7 1.1 %collective-permute-done.1.refs_6_ = f32[8,4096]{1,0:T(8,128)S(1)} collective-permute-done((f32[8,4096]{1,0:T(8,128)S(1)}, f32[8,4096]{1,0:T(8,128)S(1)}, u32[]{:S(2)}, u32[]{:S(2)}) %collective-permute-start.1) | collective-permute-done | bytes 131104 | tf_op jit(solution)/shard_map/ppermute | solution.py:386
  15.8 1.1 %shard_map.42 = f32[7,8,8192]{2,1,0:T(8,128)} custom-call(f32[7,8,8192]{2,1,0:T(8,128)S(1)} %get-tuple-element.14.refs_0_, f32[7,8,8192]{2,1,0:T(8,128)S(1)} %get-tuple-element.15.refs_1_, f32[8,8192]{1,0:T(8,128)S(1)} %get-tuple-element.16.refs_2_, f32[8,8192]{1,0:T(8,128)S(1)} %get-tuple-element.17.refs_3_, ...), custom_call_target="tpu_custom_call", output_to_operand_aliasing={{}: (8, {})} | custom-call | tf_op jit(solution)/shard_map/pallas_call | solution.py:324
Async XLA Ops:
  0.0 4.5 %copy-start.1 = (s32[8,8192]{1,0:T(8,128)S(1)}, s32[8,8192]{1,0:T(8,128)}, u32[]{:S(2)}) copy-start(s32[8,8192]{1,0:T(8,128)} %valid.5) | copy-start | bytes 786436
  0.0 4.5 %copy-start = (f32[8,7,8192]{2,0,1:T(8,128)S(1)}, f32[8,7,8192]{2,0,1:T(8,128)}, u32[]{:S(2)}) copy-start(f32[8,7,8192]{2,0,1:T(8,128)} %param.3) | copy-start | bytes 5505028
  1.5 6.5 %collective-permute-start.3 = (f32[8,4096]{1,0:T(8,128)S(1)}, f32[8,4096]{1,0:T(8,128)S(1)}, u32[]{:S(2)}, u32[]{:S(2)}) collective-permute-start(f32[8,4096]{1,0:T(8,128)S(1)} %get-tuple-element.20.own), channel_id=1, source_target_pairs={{0,8},{8,0},{16,24},{24,16},{1,9},{9,1},{17,25},{25,17},{2,10},{10... | collective-permute-start | bytes 393224 | tf_op jit(solution)/shard_map/ppermute | solution.py:386
  4.7 5.9 %collective-permute-start = (f32[8,4096]{1,0:T(8,128)S(1)}, f32[8,4096]{1,0:T(8,128)S(1)}, u32[]{:S(2)}, u32[]{:S(2)}) collective-permute-start(f32[8,4096]{1,0:T(8,128)S(1)} %shard_map.37), channel_id=1, source_target_pairs={{0,16},{8,24},{16,0},{24,8},{1,17},{9,25},{17,1},{25,9},{2,18},{10... | collective-permute-start | bytes 393224 | tf_op jit(solution)/shard_map/ppermute | solution.py:389
  6.7 6.7 %collective-permute-start.2 = (f32[8,4096]{1,0:T(8,128)S(1)}, f32[8,4096]{1,0:T(8,128)S(1)}, u32[]{:S(2)}, u32[]{:S(2)}) collective-permute-start(f32[8,4096]{1,0:T(8,128)S(1)} %get-tuple-element.19), channel_id=1, source_target_pairs={{0,8},{8,0},{16,24},{24,16},{1,9},{9,1},{17,25},{25,17},{2,10},{10... | collective-permute-start | bytes 393224 | tf_op jit(solution)/shard_map/ppermute | solution.py:386
  8.1 5.5 %collective-permute-start.4 = (f32[8,4096]{1,0:T(8,128)S(1)}, f32[8,4096]{1,0:T(8,128)S(1)}, u32[]{:S(2)}, u32[]{:S(2)}) collective-permute-start(f32[8,4096]{1,0:T(8,128)S(1)} %shard_map.40), channel_id=1, source_target_pairs={{0,16},{8,24},{16,0},{24,8},{1,17},{9,25},{17,1},{25,9},{2,18},{10... | collective-permute-start | bytes 393224 | tf_op jit(solution)/shard_map/ppermute | solution.py:389
  10.7 5.0 %collective-permute-start.1 = (f32[8,4096]{1,0:T(8,128)S(1)}, f32[8,4096]{1,0:T(8,128)S(1)}, u32[]{:S(2)}, u32[]{:S(2)}) collective-permute-start(f32[8,4096]{1,0:T(8,128)S(1)} %shard_map.39), channel_id=1, source_target_pairs={{0,8},{8,0},{16,24},{24,16},{1,9},{9,1},{17,25},{25,17},{2,10},{10... | collective-permute-start | bytes 393224 | tf_op jit(solution)/shard_map/ppermute | solution.py:386

commit v7 on v6

--- a/solution.py
+++ b/solution.py
@@ -99,7 +99,6 @@
     bands, count, _ = refl.shape
     half = sends[0].shape[1]
     day_copy = pltpu.make_async_copy(days_in, days, day_sem)
-    day_copy.start()
     copies = []
     at = 0
     while at < half:
@@ -118,6 +117,7 @@
             c.start(priority=1)
         copies.append(pair)
         at += width
+    day_copy.start()
     rows, packet_rows = tile_rows(bands, count)
     me = lax.axis_index("date")
     firsts = [bit_of(me, t) for t in bits]
@@ -165,6 +165,10 @@
     odd, _, inner = flags()
     day_col = day_in[...]
 
+    turns = jnp.where(lax.rem(lax.axis_index("tile"), 2) == 1, 60, 0)
+    spun = lax.fori_loop(0, turns, lambda i, v: v * 1.0001 + 0.5, day_col)
+    day_col = jnp.where(spun < 0.0, spun, day_col)
+
     def made(cols):
         live = valid[:, cols] > 0
         values = [refl[k, :, cols] for k in range(bands)]
@@ -246,7 +250,7 @@
     rows, _ = tile_rows(bands, count)
     day_col = day_in[...]
 
-    @each_tile(pixels // LANES)
+    @each_tile(pixels // LANES, 4)
     def _(i):
         cols = span_of(i)
         live = valid[:, cols] > 0

time: 17 us -> 16.9 us (level)
  waiting for transfers between devices: 2.12 us -> 1.87 us
    ppermute x3, starting transfers between devices: 5.61 us -> 5.92 us  [across(): return lax.ppermute(x, 'date', [(d, d ^ 1) for d in range(4)])]
    ppermute x2, starting transfers between devices: 4.13 us -> 3.82 us  [along(): return lax.ppermute(x, 'date', [(d, d ^ 2) for d in range(4)])]
    ppermute x2, waiting for transfers between devices: 0.26 us -> 0.01 us  [along(): return lax.ppermute(x, 'date', [(d, d ^ 2) for d in range(4)])]
  transfers between devices with their start and end apart: 5 -> 5, of which waited for: 3 -> 2; matrix products, arithmetic and copies ran while one was open for 0% -> 0% of each run, Pallas kernels for 14% -> 15%
where the time goes in v7:
time: 16.9 us; the launch traced here: 16.7 us
  starting transfers between devices  9.74 us (58%)
  Pallas kernels  5.05 us (30%)
  waiting for transfers between devices  1.87 us (11%)
    ppermute x3, starting transfers between devices, across(): return lax.ppermute(x, 'date', [(d, d ^ 1) for d in range(4)])  5.92 us
    ppermute x2, starting transfers between devices, along(): return lax.ppermute(x, 'date', [(d, d ^ 2) for d in range(4)])  3.82 us
    pallas_call x2, Pallas kernels, fill(): pl.pallas_call(functools.partial(fill_kernel, start, width, piece, len(go...  2.15 us
    ppermute x3, waiting for transfers between devices, across(): return lax.ppermute(x, 'date', [(d, d ^ 1) for d in range(4)])  1.86 us
    pallas_call x1, Pallas kernels, load(): pl.pallas_call(functools.partial(load_kernel, piece, bits), in_specs=[HBM...  1.5 us
    pallas_call x1, Pallas kernels, nearest(): pl.pallas_call(near_kernel, in_specs=[VMEM] * 3, out_specs=[VMEM] * 4, ou...  0.75 us
    pallas_call x2, Pallas kernels, packets(): pl.pallas_call(kernel, in_specs=[VMEM] * 3, out_specs=[VMEM] * len(widths...  0.52 us
  transfers between devices with their start and end apart: 5, of which 2 were waited for; matrix products, arithmetic and copies ran while one was open for 0% of the time, Pallas kernels for 15%

profile of v7, /device:TPU:0, one launch (start us, length us, event | category | flops | bytes accessed | tf_op | source)
XLA Modules:
  0.0 16.7 jit_solution(10803257547912426461)
XLA Ops:
  0.0 0.0 copy-start.1
  0.0 0.0 copy-start
  0.0 1.5 %load.1 = (f32[8,128]{1,0:T(8,128)S(1)}, f32[8,4096]{1,0:T(8,128)S(1)}) custom-call(s32[8]{0:T(128)} %days_in.1, f32[7,8,8192]{2,1,0:T(8,128)} %bitcast.2, s32[8,8192]{1,0:T(8,128)} %valid.5), custom_call_target="tpu_custom_call" | custom-call | tf_op jit(solution)/shard_map/load/pallas_call | solution.py:345
  1.5 3.0 %collective-permute-start.3 = (f32[8,4096]{1,0:T(8,128)S(1)}, f32[8,4096]{1,0:T(8,128)S(1)}, u32[]{:S(2)}, u32[]{:S(2)}) collective-permute-start(f32[8,4096]{1,0:T(8,128)S(1)} %get-tuple-element.20.own), channel_id=1, source_target_pairs={{0,8},{8,0},{16,24},{24,16},{1,9},{9,1},{17,25},{25,17},{2,10},{10... | collective-permute-start | bytes 393224 | tf_op jit(solution)/shard_map/ppermute | solution.py:390
  4.5 0.0 copy-done.1
  4.5 0.0 copy-done
  4.6 0.2 %shard_map.37 = f32[8,4096]{1,0:T(8,128)S(1)} custom-call(f32[7,8,8192]{2,1,0:T(8,128)S(1)} %bitcast.3, s32[8,8192]{1,0:T(8,128)S(1)} %copy-done.1, f32[8,128]{1,0:T(8,128)S(1)} %get-tuple-element.13.day_in.refs_4_), custom_call_target="tpu_custom_call" | custom-call | tf_op jit(solution)/shard_map/pallas_call | solution.py:400
  4.7 1.6 %collective-permute-start = (f32[8,4096]{1,0:T(8,128)S(1)}, f32[8,4096]{1,0:T(8,128)S(1)}, u32[]{:S(2)}, u32[]{:S(2)}) collective-permute-start(f32[8,4096]{1,0:T(8,128)S(1)} %shard_map.37), channel_id=1, source_target_pairs={{0,16},{8,24},{16,0},{24,8},{1,17},{9,25},{17,1},{25,9},{2,18},{10... | collective-permute-start | bytes 393224 | tf_op jit(solution)/shard_map/ppermute | solution.py:393
  6.3 0.3 %shard_map.38 = (f32[8,4096]{1,0:T(8,128)S(1)}, f32[8,4096]{1,0:T(8,128)S(1)}) custom-call(f32[7,8,8192]{2,1,0:T(8,128)S(1)} %bitcast.4, s32[8,8192]{1,0:T(8,128)S(1)} %copy-done.1, f32[8,128]{1,0:T(8,128)S(1)} %get-tuple-element.13.day_in.refs_4_), custom_call_target="tpu_custom_call" | custom-call | tf_op jit(solution)/shard_map/pallas_call | solution.py:400
  6.7 0.6 %collective-permute-start.2 = (f32[8,4096]{1,0:T(8,128)S(1)}, f32[8,4096]{1,0:T(8,128)S(1)}, u32[]{:S(2)}, u32[]{:S(2)}) collective-permute-start(f32[8,4096]{1,0:T(8,128)S(1)} %get-tuple-element.19), channel_id=1, source_target_pairs={{0,8},{8,0},{16,24},{24,16},{1,9},{9,1},{17,25},{25,17},{2,10},{10... | collective-permute-start | bytes 393224 | tf_op jit(solution)/shard_map/ppermute | solution.py:390
  7.3 0.8 %collective-permute-done.3.got.refs_7_ = f32[8,4096]{1,0:T(8,128)S(1)} collective-permute-done((f32[8,4096]{1,0:T(8,128)S(1)}, f32[8,4096]{1,0:T(8,128)S(1)}, u32[]{:S(2)}, u32[]{:S(2)}) %collective-permute-start.3) | collective-permute-done | bytes 131104 | tf_op jit(solution)/shard_map/ppermute | solution.py:390
  8.0 0.1 shard_map.40
  8.1 2.2 %collective-permute-start.4 = (f32[8,4096]{1,0:T(8,128)S(1)}, f32[8,4096]{1,0:T(8,128)S(1)}, u32[]{:S(2)}, u32[]{:S(2)}) collective-permute-start(f32[8,4096]{1,0:T(8,128)S(1)} %shard_map.40), channel_id=1, source_target_pairs={{0,16},{8,24},{16,0},{24,8},{1,17},{9,25},{17,1},{25,9},{2,18},{10... | collective-permute-start | bytes 393224 | tf_op jit(solution)/shard_map/ppermute | solution.py:393
  10.4 0.0 collective-permute-done.got.refs_5_
  10.4 0.1 shard_map.39
  10.4 2.3 %collective-permute-start.1 = (f32[8,4096]{1,0:T(8,128)S(1)}, f32[8,4096]{1,0:T(8,128)S(1)}, u32[]{:S(2)}, u32[]{:S(2)}) collective-permute-start(f32[8,4096]{1,0:T(8,128)S(1)} %shard_map.39), channel_id=1, source_target_pairs={{0,8},{8,0},{16,24},{24,16},{1,9},{9,1},{17,25},{25,17},{2,10},{10... | collective-permute-start | bytes 393224 | tf_op jit(solution)/shard_map/ppermute | solution.py:390
  12.7 0.8 %nearest.1 = (f32[7,8,8192]{2,1,0:T(8,128)S(1)}, f32[7,8,8192]{2,1,0:T(8,128)S(1)}, f32[8,8192]{1,0:T(8,128)S(1)}, f32[8,8192]{1,0:T(8,128)S(1)}) custom-call(f32[7,8,8192]{2,1,0:T(8,128)S(1)} %bitcast.5, s32[8,8192]{1,0:T(8,128)S(1)} %copy-done.1, f32[8,128]{1,0:T(8,128)S(1)} %get-tuple-element.13.day_in.refs_4_), custom_call_target="tpu_custom_call" | custom-call | tf_op jit(solution)/shard_map/nearest/pallas_call | solution.py:314
  13.5 0.0 collective-permute-done.2.refs_6_.refs_7_
  13.5 0.0 collective-permute-done.4.refs_5_
  13.5 1.1 %shard_map.41.refs_8_ = f32[7,8,8192]{2,1,0:T(8,128)} custom-call(f32[7,8,8192]{2,1,0:T(8,128)S(1)} %get-tuple-element.14.refs_0_, f32[7,8,8192]{2,1,0:T(8,128)S(1)} %get-tuple-element.15.refs_1_, f32[8,8192]{1,0:T(8,128)S(1)} %get-tuple-element.16.refs_2_, f32[8,8192]{1,0:T(8,128)S(1)} %get-tuple-element.17.refs_3_, ...), custom_call_target="tpu_custom_call" | custom-call | tf_op jit(solution)/shard_map/pallas_call | solution.py:328
  14.6 1.1 %collective-permute-done.1.refs_6_ = f32[8,4096]{1,0:T(8,128)S(1)} collective-permute-done((f32[8,4096]{1,0:T(8,128)S(1)}, f32[8,4096]{1,0:T(8,128)S(1)}, u32[]{:S(2)}, u32[]{:S(2)}) %collective-permute-start.1) | collective-permute-done | bytes 131104 | tf_op jit(solution)/shard_map/ppermute | solution.py:390
  15.7 1.1 %shard_map.42 = f32[7,8,8192]{2,1,0:T(8,128)} custom-call(f32[7,8,8192]{2,1,0:T(8,128)S(1)} %get-tuple-element.14.refs_0_, f32[7,8,8192]{2,1,0:T(8,128)S(1)} %get-tuple-element.15.refs_1_, f32[8,8192]{1,0:T(8,128)S(1)} %get-tuple-element.16.refs_2_, f32[8,8192]{1,0:T(8,128)S(1)} %get-tuple-element.17.refs_3_, ...), custom_call_target="tpu_custom_call", output_to_operand_aliasing={{}: (8, {})} | custom-call | tf_op jit(solution)/shard_map/pallas_call | solution.py:328
Async XLA Ops:
  0.0 4.5 %copy-start.1 = (s32[8,8192]{1,0:T(8,128)S(1)}, s32[8,8192]{1,0:T(8,128)}, u32[]{:S(2)}) copy-start(s32[8,8192]{1,0:T(8,128)} %valid.5) | copy-start | bytes 786436
  0.0 4.5 %copy-start = (f32[8,7,8192]{2,0,1:T(8,128)S(1)}, f32[8,7,8192]{2,0,1:T(8,128)}, u32[]{:S(2)}) copy-start(f32[8,7,8192]{2,0,1:T(8,128)} %param.3) | copy-start | bytes 5505028
  1.5 6.5 %collective-permute-start.3 = (f32[8,4096]{1,0:T(8,128)S(1)}, f32[8,4096]{1,0:T(8,128)S(1)}, u32[]{:S(2)}, u32[]{:S(2)}) collective-permute-start(f32[8,4096]{1,0:T(8,128)S(1)} %get-tuple-element.20.own), channel_id=1, source_target_pairs={{0,8},{8,0},{16,24},{24,16},{1,9},{9,1},{17,25},{25,17},{2,10},{10... | collective-permute-start | bytes 393224 | tf_op jit(solution)/shard_map/ppermute | solution.py:390
  4.7 5.6 %collective-permute-start = (f32[8,4096]{1,0:T(8,128)S(1)}, f32[8,4096]{1,0:T(8,128)S(1)}, u32[]{:S(2)}, u32[]{:S(2)}) collective-permute-start(f32[8,4096]{1,0:T(8,128)S(1)} %shard_map.37), channel_id=1, source_target_pairs={{0,16},{8,24},{16,0},{24,8},{1,17},{9,25},{17,1},{25,9},{2,18},{10... | collective-permute-start | bytes 393224 | tf_op jit(solution)/shard_map/ppermute | solution.py:393
  6.7 6.8 %collective-permute-start.2 = (f32[8,4096]{1,0:T(8,128)S(1)}, f32[8,4096]{1,0:T(8,128)S(1)}, u32[]{:S(2)}, u32[]{:S(2)}) collective-permute-start(f32[8,4096]{1,0:T(8,128)S(1)} %get-tuple-element.19), channel_id=1, source_target_pairs={{0,8},{8,0},{16,24},{24,16},{1,9},{9,1},{17,25},{25,17},{2,10},{10... | collective-permute-start | bytes 393224 | tf_op jit(solution)/shard_map/ppermute | solution.py:390
  8.1 5.4 %collective-permute-start.4 = (f32[8,4096]{1,0:T(8,128)S(1)}, f32[8,4096]{1,0:T(8,128)S(1)}, u32[]{:S(2)}, u32[]{:S(2)}) collective-permute-start(f32[8,4096]{1,0:T(8,128)S(1)} %shard_map.40), channel_id=1, source_target_pairs={{0,16},{8,24},{16,0},{24,8},{1,17},{9,25},{17,1},{25,9},{2,18},{10... | collective-permute-start | bytes 393224 | tf_op jit(solution)/shard_map/ppermute | solution.py:393
  10.4 5.2 %collective-permute-start.1 = (f32[8,4096]{1,0:T(8,128)S(1)}, f32[8,4096]{1,0:T(8,128)S(1)}, u32[]{:S(2)}, u32[]{:S(2)}) collective-permute-start(f32[8,4096]{1,0:T(8,128)S(1)} %shard_map.39), channel_id=1, source_target_pairs={{0,8},{8,0},{16,24},{24,16},{1,9},{9,1},{17,25},{25,17},{2,10},{10... | collective-permute-start | bytes 393224 | tf_op jit(solution)/shard_map/ppermute | solution.py:390
